TPU v7x, 32 devices: a whole 2x2x4 slice. The times are simulated.
32 devices in a mesh: shard: 4 (over z), ctx: 4 (over y, x), tp: 2 (over core).
Axes of the slice: x: 2, y: 2, z: 4, core: 2. Of those that a mesh axis runs over, the one named last changes fastest.
Arguments:
- tokens: bfloat16 [2, 4, 4096, 512], P(None, 'shard', 'ctx'), may hold values from -6 to 6
- cotangent: bfloat16 [2, 4, 4096, 512], P(None, 'shard', 'ctx'), may hold values from -6 to 6
- w_query: bfloat16 [512, 512], P('shard', 'tp'), may hold values from -0.25 to 0.25
- w_key: bfloat16 [512, 512], P('shard', 'tp'), may hold values from -0.25 to 0.25
- w_value: bfloat16 [512, 512], P('shard', 'tp'), may hold values from -0.25 to 0.25
- w_out: bfloat16 [512, 512], P('tp', 'shard'), may hold values from -6 to 6
- w_up: bfloat16 [512, 2048], P('shard', 'tp'), may hold values from -0.25 to 0.25
- w_down: bfloat16 [2048, 512], P('tp', 'shard'), may hold values from -0.125 to 0.125
- b_query: bfloat16 [8, 64], P('tp', 'shard'), may hold values from -3 to 3
- b_value: bfloat16 [8, 64], P('tp', 'shard'), may hold values from -3 to 3
- b_up: bfloat16 [8, 256], P('tp', 'shard'), may hold values from -3 to 3
- b_out: bfloat16 [512], P('shard'), may hold values from -3 to 3
- b_down: bfloat16 [512], P('shard'), may hold values from -3 to 3
- gain_attn: bfloat16 [512], P('shard'), may hold values from 0.099609375 to 1.8984375
- shift_attn: bfloat16 [512], P('shard'), may hold values from -3 to 3
- gain_ffn: bfloat16 [512], P('shard'), may hold values from 0.099609375 to 1.8984375
- shift_ffn: bfloat16 [512], P('shard'), may hold values from -3 to 3
Outputs:
- output: bfloat16 [2, 4, 4096, 512], P(None, 'shard', 'ctx')
- grad_tokens: bfloat16 [2, 4, 4096, 512], P(None, 'shard', 'ctx')
- grad_w_query: float32 [512, 512], P('shard', 'tp')
- grad_w_key: float32 [512, 512], P('shard', 'tp')
- grad_w_value: float32 [512, 512], P('shard', 'tp')
- grad_w_out: float32 [512, 512], P('tp', 'shard')
- grad_w_up: float32 [512, 2048], P('shard', 'tp')
- grad_w_down: float32 [2048, 512], P('tp', 'shard')
- grad_b_query: float32 [8, 64], P('tp', 'shard')
- grad_b_value: float32 [8, 64], P('tp', 'shard')
- grad_b_up: float32 [8, 256], P('tp', 'shard')
- grad_b_out: float32 [512], P('shard')
- grad_b_down: float32 [512], P('shard')
- grad_gain_attn: float32 [512], P('shard')
- grad_shift_attn: float32 [512], P('shard')
- grad_gain_ffn: float32 [512], P('shard')
- grad_shift_ffn: float32 [512], P('shard')
All inputs are finite; a program needn't handle non-finite values.
Results may differ from a plain program's by a relative error of at most 0.017.
Values may be sent and summed in bfloat16 or wider, within the bound.
A program may use at most 256 MiB of HBM per device.

v0:
```python
import functools
import math

import jax
import jax.numpy as jnp
from jax import lax
from jax.experimental import pallas as pl
from jax.experimental.pallas import tpu as pltpu
from jax.sharding import PartitionSpec as P

F32 = jnp.float32
BF16 = jnp.bfloat16
MESH = pl.DeviceIdType.MESH
norm_eps = 1e-05
LOG2E = math.log2(math.e)
VMEM_LIMIT = 60 * 2**20


def dot_nn(left, right):
    return lax.dot_general(left, right, (((1,), (0,)), ((), ())), preferred_element_type=F32)


def dot_nt(left, right):
    return lax.dot_general(left, right, (((1,), (1,)), ((), ())), preferred_element_type=F32)


def dot_tn(left, right):
    return lax.dot_general(left, right, (((0,), (0,)), ((), ())), preferred_element_type=F32)


def unit_norm(values):
    average = jnp.mean(values, axis=-1, keepdims=True)
    centred = values - average
    variance = jnp.mean(centred * centred, axis=-1, keepdims=True)
    inverse = lax.rsqrt(variance + norm_eps)
    return centred * inverse, inverse


def norm_back(grad_normed, unit_vals, inverse, gain):
    scaled = grad_normed * gain
    return inverse * (
        scaled
        - jnp.mean(scaled, axis=-1, keepdims=True)
        - unit_vals * jnp.mean(scaled * unit_vals, axis=-1, keepdims=True)
    )


def column_sum(values):
    return jnp.sum(values, axis=0, keepdims=True)


def full_spec(shape):
    return pl.BlockSpec(shape, lambda *_: (0,) * len(shape))


def params(limit=VMEM_LIMIT, **others):
    return pltpu.CompilerParams(vmem_limit_bytes=limit, **others)


def once(shape, index=None):
    place = index or (0,) * len(shape)
    return pl.BlockSpec(shape, lambda *_: place, pipeline_mode=pl.Buffered(1))


def send(source, target, send_sem, recv_sem, where):
    return pltpu.make_async_remote_copy(
        src_ref=source, dst_ref=target, send_sem=send_sem, recv_sem=recv_sem, device_id=where, device_id_type=MESH
    )


def gather_kernel(ns, nc, wq_ref, wk_ref, wv_ref, small_ref, x_block, w_out, small_out, x_out, *sems):
    w_send, w_recv, s_send, s_recv, x_send, x_recv, wt_send, wt_recv, st_send, st_recv, xt_send, xt_recv, local = sems
    w_refs = (wq_ref, wk_ref, wv_ref)
    kinds = range(3)
    x_ref = x_block.at[0, 0]
    s = lax.axis_index("shard")
    c = lax.axis_index("ctx")
    t = lax.axis_index("tp")
    other = 1 - t
    depth = wq_ref.shape[0]
    half = x_ref.shape[0] // 2

    barrier = pltpu.get_barrier_semaphore()
    for d in range(1, ns):
        pl.semaphore_signal(barrier, inc=1, device_id={"shard": s ^ d}, device_id_type=MESH)
    for d in range(1, nc):
        pl.semaphore_signal(barrier, inc=1, device_id={"ctx": c ^ d}, device_id_type=MESH)
    pl.semaphore_signal(barrier, inc=1, device_id={"tp": other}, device_id_type=MESH)
    pl.semaphore_wait(barrier, ns + nc - 1)

    def w_rows(part, kind, owner):
        return w_out.at[part, kind, pl.ds(pl.multiple_of(owner * depth, depth), depth), :]

    def x_rows(which):
        return x_ref.at[pl.ds(pl.multiple_of(which * half, half), half), :]

    def begin(source, target, send_sem, recv_sem, where):
        copy = send(source, target, send_sem, recv_sem, where)
        copy.start()
        return copy

    x_copies, w_copies, s_copies = {}, {}, {}
    for d in range(1, nc):
        x_copies[d] = begin(x_rows(t), x_out.at[d, 0], x_send.at[d], x_recv.at[d], {"ctx": c ^ d})
    for d in range(1, ns):
        for k in kinds:
            w_copies[d, k] = begin(
                w_refs[k], w_rows(0, k, s), w_send.at[k, d], w_recv.at[k, d], {"shard": s ^ d}
            )
        s_copies[d] = begin(small_ref, small_out.at[0, s], s_send.at[d], s_recv.at[d], {"shard": s ^ d})
    last = [begin(w_refs[k], w_rows(1, k, s), wt_send.at[k, 0], wt_recv.at[k, 0], {"tp": other}) for k in kinds]
    last.append(begin(small_ref, small_out.at[1, s], st_send.at[0], st_recv.at[0], {"tp": other}))
    locals_ = [pltpu.make_async_copy(w_refs[k], w_rows(0, k, s), local.at[k]) for k in kinds]
    locals_ += [
        pltpu.make_async_copy(small_ref, small_out.at[0, s], local.at[3]),
        pltpu.make_async_copy(x_rows(t), x_out.at[0, 0], local.at[4]),
        pltpu.make_async_copy(x_rows(other), x_out.at[0, 1], local.at[5]),
    ]
    for copy in locals_:
        copy.start()
    for d in range(1, max(ns, nc)):
        if d < ns:
            for k in kinds:
                w_copies[d, k].wait_recv()
                last.append(
                    begin(
                        w_rows(0, k, s ^ d), w_rows(1, k, s ^ d), wt_send.at[k, d], wt_recv.at[k, d], {"tp": other}
                    )
                )
            s_copies[d].wait_recv()
            last.append(
                begin(small_out.at[0, s ^ d], small_out.at[1, s ^ d], st_send.at[d], st_recv.at[d], {"tp": other})
            )
        if d < nc:
            x_copies[d].wait_recv()
            last.append(begin(x_out.at[d, 0], x_out.at[d, 1], xt_send.at[d], xt_recv.at[d], {"tp": other}))
    for copies in (x_copies, w_copies, s_copies):
        for copy in copies.values():
            copy.wait_send()
    for copy in last:
        copy.wait()
    for copy in locals_:
        copy.wait()


def gather_first(weights, small, tokens, ns, nc):
    depth, width = weights[0].shape
    length, features = tokens.shape[2:]
    dma = pltpu.SemaphoreType.DMA
    vmem = pl.BlockSpec(memory_space=pltpu.VMEM)
    return pl.pallas_call(
        functools.partial(gather_kernel, ns, nc),
        grid=(1,),
        in_specs=[vmem] * 4 + [once((1, 1, length, features))],
        out_specs=[pl.BlockSpec(memory_space=pl.ANY)] * 3,
        out_shape=[
            jax.ShapeDtypeStruct((2, 3, ns * depth, width), BF16),
            jax.ShapeDtypeStruct((2, ns) + small.shape, BF16),
            jax.ShapeDtypeStruct((nc, 2, length // 2, features), BF16),
        ],
        scratch_shapes=[dma((3, ns)), dma((3, ns)), dma((ns,)), dma((ns,)), dma((nc,)), dma((nc,))]
        + [dma((3, ns)), dma((3, ns)), dma((ns,)), dma((ns,)), dma((nc,)), dma((nc,)), dma((6,))],
        compiler_params=params(collective_id=0, has_side_effects=True),
        name="gather_first",
    )(*weights, small, tokens)


def front_kernel(x_ref, w_ref, vec_ref, bias_ref, n_ref, k_ref, v_ref, q_ref, *, q_scale):
    step = pl.program_id(0)
    gain, shift = vec_ref[2:3], vec_ref[3:4]
    width = w_ref.shape[3]
    size = x_ref.shape[0] // 4
    for i in range(4):
        rows = slice(i * size, (i + 1) * size)
        unit, _ = unit_norm(x_ref[rows].astype(F32))
        normed = (unit * gain + shift).astype(BF16)
        n_ref[rows] = normed
        for part in range(2):
            cols = slice(part * width, (part + 1) * width)
            k_ref[rows, cols] = dot_nn(normed, w_ref[part, 1]).astype(BF16)
            v_ref[rows, cols] = (dot_nn(normed, w_ref[part, 2]) + bias_ref[1:2, cols]).astype(BF16)

    @pl.when(step == 0)
    def _():
        normed = n_ref[: q_ref.shape[0]]
        for part in range(2):
            cols = slice(part * width, (part + 1) * width)
            q_ref[:, cols] = ((dot_nn(normed, w_ref[part, 0]) + bias_ref[0:1, cols]) * q_scale).astype(BF16)


def front(x_all, weights, vectors, biases, head_width, half):
    keys, features = x_all.shape
    block = 2 * half
    width = 2 * weights.shape[3]
    return pl.pallas_call(
        functools.partial(front_kernel, q_scale=LOG2E / math.sqrt(head_width)),
        grid=(keys // block,),
        in_specs=[
            pl.BlockSpec((block, features), lambda i: (i, 0)),
            once(weights.shape),
            once(vectors.shape),
            once(biases.shape),
        ],
        out_specs=[
            pl.BlockSpec((block, features), lambda i: (i, 0)),
            pl.BlockSpec((block, width), lambda i: (i, 0)),
            pl.BlockSpec((block, width), lambda i: (i, 0)),
            full_spec((half, width)),
        ],
        out_shape=[
            jax.ShapeDtypeStruct((keys, features), BF16),
            jax.ShapeDtypeStruct((keys, width), BF16),
            jax.ShapeDtypeStruct((keys, width), BF16),
            jax.ShapeDtypeStruct((half, width), BF16),
        ],
        compiler_params=params(),
        cost_estimate=pl.CostEstimate(
            flops=4 * keys * features * width, bytes_accessed=8 * keys * features, transcendentals=keys
        ),
        name="front",
    )(x_all, weights, vectors, biases)


def with_parts(lane, base, values, first, width):
    high = values.astype(BF16).astype(F32)
    rest = values - high
    middle = rest.astype(BF16).astype(F32)
    low = rest - middle
    extra = jnp.where(
        lane == first, high, jnp.where(lane == first + 1, middle, jnp.where(lane == first + 2, low, 0.0))
    )
    inside = (lane < width) if first else (lane >= width)
    return jnp.where(inside, base, extra)


def greet(counts):
    barrier = pltpu.get_barrier_semaphore()
    total = 0
    for name, count in counts:
        me = lax.axis_index(name)
        for d in range(1, count):
            pl.semaphore_signal(barrier, inc=1, device_id={name: me ^ d}, device_id_type=MESH)
            total += 1
    pl.semaphore_wait(barrier, total)


class Gather:

    def __init__(self, name, count, source, theirs, target, place, sems):
        self.name, self.count, self.source, self.theirs = name, count, source, theirs
        self.target, self.place = target, place
        self.out_sem, self.in_sem, self.cross_out, self.cross_in, self.local = sems
        self.me = lax.axis_index(name)

    def first(self, d):
        where = {self.name: self.me ^ d}
        return send(self.source, self.place(self.target, 0, self.me, d), self.out_sem.at[d], self.in_sem.at[d], where)

    def cross(self, d):
        where = {"tp": 1 - lax.axis_index("tp")}
        owner = self.me ^ d
        source = self.place(self.target, 0, owner, d) if d else self.source
        return send(source, self.place(self.target, 1, owner, d), self.cross_out.at[d], self.cross_in.at[d], where)

    def locals(self):
        copies = [pltpu.make_async_copy(self.source, self.place(self.target, 0, self.me, 0), self.local.at[0])]
        if self.theirs is not None:
            copies.append(pltpu.make_async_copy(self.theirs, self.place(self.target, 1, self.me, 0), self.local.at[1]))
        return copies

    def crossed(self):
        return range(0 if self.theirs is None else 1, self.count)

    def start(self):
        for d in range(1, self.count):
            self.first(d).start()
        for copy in self.locals():
            copy.start()
        if self.theirs is None:
            self.cross(0).start()

    def forward(self):
        for d in range(1, self.count):
            self.first(d).wait_recv()
            self.cross(d).start()

    def finish(self):
        for d in range(1, self.count):
            self.first(d).wait_send()
        for d in self.crossed():
            self.cross(d).wait()
        for copy in self.locals():
            copy.wait()


def place_rows(ref, part, owner, d):
    size = ref.shape[1] // lax.axis_size("shard")
    return ref.at[part, pl.ds(pl.multiple_of(owner * size, size), size), :]


def place_columns(ref, part, owner, d):
    size = ref.shape[2] // lax.axis_size("shard")
    return ref.at[part, :, pl.ds(pl.multiple_of(owner * size, size), size)]


def place_slot(ref, part, owner, d):
    return ref.at[part, owner]


def place_distance(ref, part, owner, d):
    return ref.at[d, part]


def gather_sems(count):
    dma = pltpu.SemaphoreType.DMA
    return [dma((count,)), dma((count,)), dma((count,)), dma((count,)), dma((2,))]


def attend_kernel(*refs, kc, width, plans):
    count = len(plans)
    q_ref, k_ref, v_ref = refs[:3]
    sources = refs[3 : 3 + count]
    o_ref, qx_ref = refs[3 + count : 5 + count]
    targets = refs[5 + count : 5 + 2 * count]
    scores = refs[5 + 2 * count]
    sems = refs[6 + 2 * count :]
    step = pl.program_id(0)
    last = pl.num_programs(0) - 1
    t = lax.axis_index("tp")

    def gathers(wanted):
        found = []
        for i, (name, number, place, split) in enumerate(plans):
            if name != wanted:
                continue
            source, theirs = sources[i], None
            if split:
                source = source.at[0, 0]
                half = source.shape[0] // 2
                theirs = source.at[pl.ds(pl.multiple_of((1 - t) * half, half), half), :]
                source = source.at[pl.ds(pl.multiple_of(t * half, half), half), :]
            found.append(Gather(name, number, source, theirs, targets[i], place, sems[5 * i : 5 * i + 5]))
        return found

    counts = {name: number for name, number, _, _ in plans}

    @pl.when(step == 0)
    def _():
        greet([("tp", 2)] + list(counts.items()))
        for name in counts:
            for gather in gathers(name):
                gather.start()

    @pl.when(step == last)
    def _():
        for gather in gathers("ctx"):
            gather.forward()

    rows, lanes = q_ref.shape
    keys = k_ref.shape[0]
    lane = lax.broadcasted_iota(jnp.int32, (rows, lanes), 1)
    lane_v = lax.broadcasted_iota(jnp.int32, (kc, lanes), 1)
    q = q_ref[...].astype(F32)
    tops = []
    for h in range(2):
        inside = (lane < width) if h == 0 else (lane >= width)
        q_head = jnp.where(inside, q, 0.0).astype(BF16)
        top = None
        for i in range(keys // kc):
            part = dot_nt(k_ref[i * kc : (i + 1) * kc], q_head)
            scores[h, i * kc : (i + 1) * kc] = part
            here = jnp.max(part.reshape(kc // 8, 8, rows), axis=0)
            top = here if top is None else jnp.maximum(top, here)
        tops.append(jnp.max(top, axis=0, keepdims=True))
    outs = []
    for h in range(2):
        inside_v = (lane_v < width) if h == 0 else (lane_v >= width)
        total = jnp.zeros((lanes, rows), F32)
        for i in range(keys // kc):
            v_one = jnp.where(inside_v, v_ref[i * kc : (i + 1) * kc], jnp.ones((), BF16))
            exponent = jnp.exp2(scores[h, i * kc : (i + 1) * kc] - tops[h]).astype(BF16)
            total += dot_tn(v_one, exponent)
        first = width if h == 0 else 0
        log_total = tops[h] + jnp.log2(total[first : first + 1, :])
        total = total.T
        outs.append(total / pltpu.roll(total, width, 1))
        log_column = jnp.broadcast_to(log_total, (8, rows)).T[:, :1]
        qx_ref[:, h * lanes : (h + 1) * lanes] = with_parts(lane, q, -log_column, first, width).astype(BF16)
    o_ref[...] = jnp.where(lane < width, outs[0], outs[1]).astype(BF16)

    @pl.when(step == last)
    def _():
        for gather in gathers("shard"):
            gather.forward()
        for name in counts:
            for gather in gathers(name):
                gather.finish()


def attend_forward(q, k, v, width, plans, sources, source_specs, shapes, number):
    rows, cols = q.shape
    keys = k.shape[0]
    lanes = 2 * width
    kc = 512
    anywhere = pl.BlockSpec(memory_space=pl.ANY)
    return pl.pallas_call(
        functools.partial(attend_kernel, kc=kc, width=width, plans=plans),
        grid=(cols // lanes,),
        in_specs=[
            pl.BlockSpec((rows, lanes), lambda j: (0, j)),
            pl.BlockSpec((keys, lanes), lambda j: (0, j)),
            pl.BlockSpec((keys, lanes), lambda j: (0, j)),
        ]
        + source_specs,
        out_specs=[
            pl.BlockSpec((rows, lanes), lambda j: (0, j)),
            pl.BlockSpec((rows, 2 * lanes), lambda j: (0, j)),
        ]
        + [anywhere] * len(plans),
        out_shape=[
            jax.ShapeDtypeStruct((rows, cols), BF16),
            jax.ShapeDtypeStruct((rows, 2 * cols), BF16),
        ]
        + [jax.ShapeDtypeStruct(shape, BF16) for shape in shapes],
        scratch_shapes=[pltpu.VMEM((2, keys, rows), F32)]
        + [sem for plan in plans for sem in gather_sems(plan[1])],
        compiler_params=params(collective_id=number, has_side_effects=True),
        cost_estimate=pl.CostEstimate(
            flops=12 * rows * keys * cols, bytes_accessed=4 * keys * cols, transcendentals=rows * keys * cols // width
        ),
        name="attend_forward",
    )(q, k, v, *sources)


def sum_rows(target, at, left, left_at, right, right_at, rows, chunk=64):
    def one(i, carry):
        here = pl.multiple_of(i * chunk, chunk)
        value = left[pl.ds(left_at + here, chunk), :].astype(F32) + right[pl.ds(right_at + here, chunk), :].astype(F32)
        target[pl.ds(at + here, chunk), :] = value.astype(target.dtype)
        return carry

    lax.fori_loop(0, rows // chunk, one, 0)


class Axis:

    def __init__(self, name, count, sems):
        self.name, self.count, self.sems = name, count, sems
        self.me = lax.axis_index(name)

    def copy(self, d, source, target):
        return send(source(self.me ^ d, d), target(self.me, d), self.sems[0].at[d], self.sems[1].at[d], {self.name: self.me ^ d})

    def start(self, source, target):
        for d in range(1, self.count):
            self.copy(d, source, target).start()

    def wait(self, source, target):
        for d in range(1, self.count):
            self.copy(d, source, target).wait()


def axis_sems(*counts):
    return [pltpu.SemaphoreType.DMA((count,)) for count in counts for _ in range(2)]


def cross(source, target, sems, i):
    return send(source, target, sems[0].at[i], sems[1].at[i], {"tp": 1 - lax.axis_index("tp")})


class RowSum:

    def __init__(self, dw_send, dw_own, extra, received, total, blocks, tp_sems, ctx):
        self.dw_send, self.dw_own, self.extra = dw_send, dw_own, extra
        self.received, self.total, self.blocks = received, total, blocks
        self.tp_sems, self.ctx = tp_sems, ctx
        self.main, self.more = dw_own.shape[0], extra.shape[1]
        self.size = (self.main + self.more) // ctx.count

    def crossing(self):
        return [
            cross(self.dw_send, self.received.at[pl.ds(0, self.main), :], self.tp_sems, 0),
            cross(self.extra.at[1], self.received.at[pl.ds(self.main, self.more), :], self.tp_sems, 1),
        ]

    def start(self):
        for copy in self.crossing():
            copy.start()

    def source(self, peer, d):
        return self.total.at[pl.ds(pl.multiple_of(peer * self.size, 16), self.size), :]

    def target(self, me, d):
        return self.blocks.at[d]

    def spread(self):
        for copy in self.crossing():
            copy.wait()
        sum_rows(self.total, 0, self.dw_own, 0, self.received, 0, self.main)
        sum_rows(self.total, self.main, self.extra.at[0], 0, self.received, self.main, self.more)
        self.ctx.start(self.source, self.target)

    def finish(self, out):
        self.ctx.wait(self.source, self.target)
        count, size, width = out.shape
        value = self.total[pl.ds(pl.multiple_of(self.ctx.me * self.size, 16), self.size), :].astype(F32)
        for d in range(1, self.ctx.count):
            value += self.blocks[d].astype(F32)
        for j in range(count):
            out[j] = value[:, j * width : (j + 1) * width].astype(out.dtype)


class ShardSum:

    def __init__(self, parts, received, blocks, shard, ctx):
        self.parts, self.received, self.blocks, self.shard, self.ctx = parts, received, blocks, shard, ctx

    def source(self, peer, d):
        return self.parts.at[peer]

    def target(self, me, d):
        return self.received.at[d]

    def start(self):
        self.shard.start(self.source, self.target)

    def mine(self, peer, d):
        return self.blocks.at[self.ctx.me]

    def theirs(self, me, d):
        return self.blocks.at[me]

    def spread(self):
        self.shard.wait(self.source, self.target)
        value = self.parts[self.shard.me].astype(F32)
        for d in range(1, self.shard.count):
            value += self.received[d].astype(F32)
        self.blocks[self.ctx.me] = value.astype(BF16)
        self.ctx.start(self.mine, self.theirs)

    def finish(self):
        self.ctx.wait(self.mine, self.theirs)


class InputSum:

    def __init__(self, dn_send, dn_own, received, total, blocks, tp_sems, ctx):
        self.dn_send, self.dn_own, self.received = dn_send, dn_own, received
        self.total, self.blocks, self.tp_sems, self.ctx = total, blocks, tp_sems, ctx

    def crossing(self, d):
        return cross(self.dn_send(d), self.received.at[d], self.tp_sems, d)

    def source(self, peer, d):
        return self.total.at[d]

    def target(self, me, d):
        return self.blocks.at[d]

    def spread_one(self, d):
        self.crossing(d).wait()
        sum_rows(self.total.at[d], 0, self.dn_own(d), 0, self.received.at[d], 0, self.received.shape[1])
        if d:
            self.ctx.copy(d, self.source, self.target).start()

    def finish(self):
        self.ctx.wait(self.source, self.target)

    def rows(self, at, size):
        value = self.total[0, pl.ds(at, size), :].astype(F32)
        for d in range(1, self.ctx.count):
            value += self.blocks[d, pl.ds(at, size), :].astype(F32)
        return value


def attend_back_step(refs, scratch, starts, width):
    qx_ref, k_ref, v_ref, go_ref, o_ref, n_ref, x_ref, w_ref = refs
    gx_all, dq_acc, dn_acc, dw_acc, db_ref, sums_ref = scratch
    i, j = pl.program_id(0), pl.program_id(1)
    last_block, last_pair = pl.num_programs(0) - 1, pl.num_programs(1) - 1
    rows, lanes = o_ref.shape
    keys = k_ref.shape[0]
    lane = lax.broadcasted_iota(jnp.int32, (rows, lanes), 1)
    lane_k = lax.broadcasted_iota(jnp.int32, (keys, lanes), 1)
    one = jnp.ones((), BF16)

    @pl.when(i == 0)
    def _():
        grad_out = go_ref[...].astype(F32)
        both = grad_out * o_ref[...].astype(F32)
        for h in range(2):
            inside = (lane < width) if h == 0 else (lane >= width)
            delta = jnp.sum(jnp.where(inside, both, 0.0), axis=1, keepdims=True)
            gx_all[j, h] = with_parts(lane, grad_out, -delta, width if h == 0 else 0, width).astype(BF16)
        dq_acc[j] = jnp.zeros(dq_acc.shape[1:], F32)
        dw_acc[j] = starts[0][j] if starts else jnp.zeros(dw_acc.shape[1:], F32)
        db_ref[j] = starts[1][j] if starts else jnp.zeros(db_ref.shape[1:], F32)

    @pl.when((i == 0) & (j == 0))
    def _():
        sums_ref[...] = starts[2][...] if starts else jnp.zeros_like(sums_ref)

    @pl.when(j == 0)
    def _():
        dn_acc[...] = jnp.zeros_like(dn_acc)

    grad_k, grad_v, grad_q = [], [], []
    for h in range(2):
        inside_k = (lane_k < width) if h == 0 else (lane_k >= width)
        kx = jnp.where(inside_k, k_ref[...], one)
        vx = jnp.where(inside_k, v_ref[...], one)
        qx = qx_ref[:, h * lanes : (h + 1) * lanes]
        gx = gx_all[j, h]
        prob = jnp.exp2(dot_nt(kx, qx))
        grad_v.append(dot_nn(prob.astype(BF16), gx))
        grad_score = (prob * dot_nt(vx, gx)).astype(BF16)
        grad_k.append(dot_nn(grad_score, qx))
        grad_q.append(dot_tn(kx, grad_score))
    dk = (jnp.where(lane_k < width, grad_k[0], grad_k[1]) * (1.0 / LOG2E)).astype(BF16)
    dv = jnp.where(lane_k < width, grad_v[0], grad_v[1]).astype(BF16)
    dq_acc[j] += jnp.concatenate([grad_q[0][:width], grad_q[1][width:]], axis=0)
    both = jnp.concatenate([dk, dv], axis=1)
    weights = jnp.concatenate([w_ref[0, 1], w_ref[0, 2]], axis=1)
    dn_acc[...] += dot_nt(both, weights)
    grad_w = dot_tn(both, n_ref[...])
    dw_acc[j, 1] += grad_w[:lanes]
    dw_acc[j, 2] += grad_w[lanes:]
    db_ref[j, 1:2] += column_sum(dv.astype(F32))

    @pl.when(i == last_block)
    def _():
        dq = (dq_acc[j].T * (1.0 / math.sqrt(width))).astype(BF16)
        dn_acc[:rows] += dot_nt(dq, w_ref[0, 0])
        dw_acc[j, 0] += dot_tn(dq, n_ref[:rows])
        db_ref[j, 0:1] += column_sum(dq.astype(F32))

    @pl.when(j == last_pair)
    def _():
        unit, _ = unit_norm(x_ref[...].astype(F32))
        sums_ref[0:1] += column_sum(dn_acc[...] * unit)
        sums_ref[1:2] += column_sum(dn_acc[...])


def attend_back_kernel(*refs, width, nc, ns, hosted, hosted_counts, started):
    i, j = pl.program_id(0), pl.program_id(1)
    last_pair = pl.num_programs(1) - 1
    n_in, n_out, n_scratch = hosted_counts
    at = 8
    base = refs[:at]
    starts = refs[at : at + 3] if started else ()
    at += 3 if started else 0
    extra_in, at = refs[at : at + n_in], at + n_in
    (dw_ref, db_ref, sums_ref, dn_done), at = refs[at : at + 4], at + 4
    extra_out, at = refs[at : at + n_out], at + n_out
    gx_all, dq_acc, dn_acc, dw_acc, dn_sent, dn_received, dn_total, dn_blocks, tp_out, tp_in, ctx_out, ctx_in = refs[at : at + 12]
    extra_scratch = refs[at + 12 :]
    inputs = InputSum(
        lambda d: dn_sent.at[d, 1], lambda d: dn_sent.at[d, 0], dn_received, dn_total, dn_blocks,
        (tp_out, tp_in), Axis("ctx", nc, (ctx_out, ctx_in)),
    )
    guest = hosted(extra_in, extra_out, extra_scratch, nc, ns)

    @pl.when((i == 0) & (j == 0))
    def _():
        greet(guest.peers)
        guest.begin()

    @pl.when((i == 1) & (j == 0))
    def _():
        guest.middle()

    for d in range(1, nc):

        @pl.when((i == nc - d) & (j == 0))
        def _(d=d):
            inputs.crossing(d).start()

        @pl.when((i == nc - d) & (j == last_pair - 1))
        def _(d=d):
            inputs.spread_one(d)

    attend_back_step(
        base, (gx_all, dq_acc, dn_acc, dw_acc, db_ref, sums_ref), starts, width
    )

    @pl.when(j == last_pair)
    def _():
        half = dn_acc.shape[0] // 2
        for part in range(2):
            dn_sent[nc - 1 - i, part] = dn_acc[part * half : (part + 1) * half].astype(BF16)

    @pl.when((i == nc - 1) & (j == last_pair))
    def _():
        dw_ref[...] = dw_acc[...].astype(dw_ref.dtype)
        inputs.crossing(0).start()
        guest.end()
        inputs.spread_one(0)
        inputs.finish()
        size = 64

        def one(r, carry):
            here = pl.multiple_of(r * size, size)
            dn_done[pl.ds(here, size), :] = inputs.rows(here, size)
            return carry

        lax.fori_loop(0, dn_done.shape[0] // size, one, 0)


class HostRows:

    def __init__(self, ins, outs, scratch, nc, ns):
        dw_all, dw_own, extra, out_half = ins
        self.dw_out, whole = outs
        received, total, blocks, tp_out, tp_in, ctx_out, ctx_in, sems = scratch
        t = lax.axis_index("tp")
        self.rows = RowSum(
            dw_all.at[1], dw_own.at[0], extra, received, total, blocks, (tp_out, tp_in), Axis("ctx", nc, (ctx_out, ctx_in))
        )
        self.copies = lambda: [
            cross(out_half, whole.at[:, t], (sems, sems.at[pl.ds(1, 1)]), 0),
            pltpu.make_async_copy(out_half, whole.at[:, t], sems.at[2]),
        ]
        self.peers = [("tp", 2), ("ctx", nc)]

    def begin(self):
        self.rows.start()
        for copy in self.copies():
            copy.start()

    def middle(self):
        self.rows.spread()

    def end(self):
        self.rows.finish(self.dw_out)
        for copy in self.copies():
            copy.wait()


class HostShards:

    def __init__(self, ins, outs, scratch, nc, ns):
        (self.done,) = outs
        received, self.blocks, z_out, z_in, back_out, back_in = scratch
        self.sums = ShardSum(
            ins[0], received, self.blocks, Axis("shard", ns, (z_out, z_in)), Axis("ctx", nc, (back_out, back_in))
        )
        self.peers = [("tp", 2), ("ctx", nc), ("shard", ns)]

    def begin(self):
        self.sums.start()

    def middle(self):
        self.sums.spread()

    def end(self):
        self.sums.finish()
        self.done[...] = self.blocks[...]


def attend_back(
    hosted, entry, grad_mixed, x_all, weights, width, micro, starts, kind, ins, in_specs, outs, out_specs, scratch, number, ns, nc
):
    normed, k, v, qx, mixed = entry
    rows, cols = mixed.shape
    keys, features = normed.shape
    lanes = 2 * width
    pairs = cols // lanes
    size = keys // nc
    each = pairs // 2
    stack = (pairs, 3, lanes, features)
    block = pltpu.VMEM((nc, rows, features), BF16)

    def key_block(shape, column):
        return pl.BlockSpec(shape, lambda i, j: (nc - 1 - i, j if column else 0))

    return pl.pallas_call(
        functools.partial(
            attend_back_kernel, width=width, nc=nc, ns=ns, hosted=hosted,
            hosted_counts=(len(ins), len(outs), len(scratch)), started=bool(starts),
        ),
        grid=(nc, pairs),
        in_specs=[
            pl.BlockSpec((rows, 2 * lanes), lambda i, j: (0, j)),
            key_block((size, lanes), True),
            key_block((size, lanes), True),
            pl.BlockSpec((rows, lanes), lambda i, j: (micro, j)),
            pl.BlockSpec((rows, lanes), lambda i, j: (0, j)),
            key_block((size, features), False),
            key_block((size, features), False),
            pl.BlockSpec((1, 3, features, lanes), lambda i, j: (j // each, 0, 0, j % each)),
        ]
        + [once(start.shape) for start in starts]
        + in_specs,
        out_specs=[full_spec(stack), full_spec((pairs, 8, lanes)), full_spec((8, features)), full_spec((rows, features))]
        + out_specs,
        out_shape=[
            jax.ShapeDtypeStruct(stack, kind),
            jax.ShapeDtypeStruct((pairs, 8, lanes), F32),
            jax.ShapeDtypeStruct((8, features), F32),
            jax.ShapeDtypeStruct((rows, features), F32),
        ]
        + outs,
        scratch_shapes=[
            pltpu.VMEM((pairs, 2, rows, lanes), BF16),
            pltpu.VMEM((pairs, lanes, rows), F32),
            pltpu.VMEM((size, features), F32),
            pltpu.VMEM(stack, F32),
            pltpu.VMEM((nc, 2, rows, features), BF16),
            block, block, block,
            *axis_sems(nc, nc),
        ]
        + scratch,
        compiler_params=params(collective_id=number, has_side_effects=True),
        cost_estimate=pl.CostEstimate(
            flops=30 * rows * keys * cols, bytes_accessed=8 * keys * cols, transcendentals=rows * keys * cols // width
        ),
        name="attend_back",
    )(qx, k, v, grad_mixed, mixed, normed, x_all, weights, *starts, *ins)


def attend_back_rows(entry, grad_mixed, x_all, weights, width, dw, extra, out, ns, nc):
    main, features = dw.shape[1:]
    rows = main + extra.shape[1]
    block = (nc, rows // nc, features)
    parts = (ns, rows // nc, features // ns)
    micros, half, _ = out.shape
    anywhere = pl.BlockSpec(memory_space=pl.ANY)
    return attend_back(
        HostRows, entry, grad_mixed, x_all, weights, width, 0, (), F32,
        [dw, dw, extra, out],
        [anywhere, once((1, main, features)), once(extra.shape), once(out.shape)],
        [jax.ShapeDtypeStruct(parts, BF16), jax.ShapeDtypeStruct((micros, 2, half, features), BF16)],
        [full_spec(parts), anywhere],
        [
            pltpu.VMEM((rows, features), BF16), pltpu.VMEM((rows, features), BF16), pltpu.VMEM(block, BF16),
            *axis_sems(2, nc), pltpu.SemaphoreType.DMA((3,)),
        ],
        3, ns, nc,
    )


def attend_back_shards(entry, grad_mixed, x_all, weights, width, starts, dw_parts, ns, nc):
    _, size, part = dw_parts.shape
    return attend_back(
        HostShards, entry, grad_mixed, x_all, weights, width, 1, starts, BF16,
        [dw_parts], [once(dw_parts.shape)],
        [jax.ShapeDtypeStruct((nc, size, part), BF16)], [full_spec((nc, size, part))],
        [pltpu.VMEM(dw_parts.shape, BF16), pltpu.VMEM((nc, size, part), BF16), *axis_sems(ns, nc)],
        4, ns, nc,
    )


def ffn_kernel(
    where_ref, x_ref, o0_ref, o1_ref, g_ref, w_out, w_up, w_down, bup_ref, vec_ref,
    out_ref, gm_ref, gx_ref, dw_ref, dup_ref, dvec_ref, dw_acc,
):
    step = pl.program_id(0)
    steps = pl.num_programs(0)
    b_out, b_down, gain, shift = (vec_ref[i : i + 1, :] for i in (0, 1, 4, 5))
    hw = w_out.shape[1]
    hidden = w_up.shape[2]

    @pl.when(step == 0)
    def _():
        dw_acc[...] = jnp.zeros_like(dw_acc)
        dup_ref[...] = jnp.zeros_like(dup_ref)
        dvec_ref[...] = jnp.zeros_like(dvec_ref)

    mixed = jnp.where(2 * step < steps, o0_ref[...], o1_ref[...])
    grad_b = g_ref[0, 0]
    grad = grad_b.astype(F32)
    attended = dot_nn(mixed[:, :hw], w_out[0]) + dot_nn(mixed[:, hw:], w_out[1])
    middle = x_ref[0, 0].astype(F32) + (attended + b_out)
    unit, inverse = unit_norm(middle)
    normed = (unit * gain + shift).astype(BF16)
    ffn_out = jnp.zeros_like(middle)
    grad_normed = jnp.zeros_like(middle)
    for part in range(2):
        pre = dot_nn(normed, w_up[part]) + bup_ref[part]
        gate = 0.5 + 0.5 * lax.erf(pre * math.sqrt(0.5))
        active = (pre * gate).astype(BF16)
        ffn_out += dot_nn(active, w_down[part])
        slope = gate + pre * jnp.exp(pre * pre * -0.5) * (1.0 / math.sqrt(2.0 * math.pi))
        grad_pre_f = dot_nt(grad_b, w_down[part]) * slope
        grad_pre = grad_pre_f.astype(BF16)
        dup_ref[part] += column_sum(grad_pre.astype(F32))
        grad_normed += dot_nt(grad_pre, w_up[part])
        dw_acc[part, hw : hw + hidden] += dot_tn(active, grad_b)
        dw_acc[part, hw + hidden :] += dot_tn(grad_pre, normed)
    out_ref[...] = (middle + (ffn_out + b_down)).astype(BF16)
    grad_middle = grad + norm_back(grad_normed, unit, inverse, gain)
    gm_ref[...] = grad_middle
    grad_att = grad_middle.astype(BF16)
    dvec_ref[0:1] += column_sum(grad_att.astype(F32))
    dvec_ref[1:2] += column_sum(grad)
    dvec_ref[2:3] += column_sum(grad_normed * unit)
    dvec_ref[3:4] += column_sum(grad_normed)
    for part in range(2):
        cols = slice(part * hw, (part + 1) * hw)
        gx_ref[:, cols] = dot_nt(grad_att, w_out[part]).astype(BF16)
        dw_acc[part, :hw] += dot_tn(mixed[:, cols], grad_att)

    @pl.when(step == steps - 1)
    def _():
        dw_ref[...] = dw_acc[...].astype(BF16)


def feed_forward(tokens, mixed, cotangent, w_out, w_up, w_down, b_up, vectors, where):
    micros, _, length, features = tokens.shape
    block = 256
    half = length // 2
    each = half // block
    rows = micros * half
    hw, hidden = w_out.shape[1], w_up.shape[2]
    total = hw + 2 * hidden
    row_spec = pl.BlockSpec((block, features), lambda i, t: (i, 0))
    input_spec = pl.BlockSpec((1, 1, block, features), lambda i, t: (i // each, 0, t[0] * each + i % each, 0))
    return pl.pallas_call(
        ffn_kernel,
        grid_spec=pltpu.PrefetchScalarGridSpec(
            num_scalar_prefetch=1,
            grid=(rows // block,),
            in_specs=[
                input_spec,
                pl.BlockSpec((block, 2 * hw), lambda i, t: (jnp.minimum(i, each - 1), 0)),
                pl.BlockSpec((block, 2 * hw), lambda i, t: (jnp.maximum(i - each, 0), 0)),
                input_spec,
            ]
            + [once(w.shape) for w in (w_out, w_up, w_down)]
            + [once(b_up.shape), once(vectors.shape)],
            out_specs=[row_spec] * 3
            + [full_spec((2, total, features)), full_spec((2, 1, hidden)), full_spec((8, features))],
            scratch_shapes=[pltpu.VMEM((2, total, features), F32)],
        ),
        out_shape=[
            jax.ShapeDtypeStruct((rows, features), BF16),
            jax.ShapeDtypeStruct((rows, features), F32),
            jax.ShapeDtypeStruct((rows, 2 * hw), BF16),
            jax.ShapeDtypeStruct((2, total, features), BF16),
            jax.ShapeDtypeStruct((2, 1, hidden), F32),
            jax.ShapeDtypeStruct((8, features), F32),
        ],
        compiler_params=params(),
        cost_estimate=pl.CostEstimate(
            flops=12 * rows * total * features, bytes_accessed=20 * total * features, transcendentals=4 * rows * hidden
        ),
        name="feed_forward",
    )(where, tokens, *mixed, cotangent, w_out, w_up, w_down, b_up, vectors)


def last_kernel(
    dw_ref, extra_ref, dn0_ref, dn1_ref, x_ref, gm_ref, vec_ref,
    grad_ref, blocks_ref,
    w_received, w_total, w_blocks, z_parts, z_received,
    wtp_out, wtp_in, wctx_out, wctx_in, z_out, z_in, back_out, back_in, row_out, row_in, *, ns, nc,
):
    t = lax.axis_index("tp")
    half = grad_ref.shape[2]
    rows = RowSum(
        dw_ref.at[1], dw_ref.at[0], extra_ref, w_received, w_total, w_blocks, (wtp_out, wtp_in),
        Axis("ctx", nc, (wctx_out, wctx_in)),
    )
    weights = ShardSum(
        z_parts, z_received, blocks_ref, Axis("shard", ns, (z_out, z_in)), Axis("ctx", nc, (back_out, back_in))
    )

    def row(micro):
        return cross(grad_ref.at[micro, t], grad_ref.at[micro, t], (row_out, row_in), micro)

    def finish_rows(micro, dn_ref):
        size = 64

        def one(i, carry):
            at = pl.multiple_of(i * size, size)
            unit, inverse = unit_norm(x_ref[micro, 0, pl.ds(t * half + at, size), :].astype(F32))
            value = gm_ref[micro, pl.ds(at, size), :] + norm_back(
                dn_ref[pl.ds(at, size), :], unit, inverse, vec_ref[2:3]
            )
            grad_ref[micro, t, pl.ds(at, size), :] = value.astype(BF16)
            return carry

        lax.fori_loop(0, half // size, one, 0)
        row(micro).start()

    greet([("tp", 2), ("ctx", nc), ("shard", ns)])
    rows.start()
    rows.spread()
    finish_rows(0, dn0_ref)
    rows.finish(z_parts)
    weights.start()
    finish_rows(1, dn1_ref)
    weights.spread()
    weights.finish()
    for micro in range(2):
        row(micro).wait()


def last_sums(dw, extra, dn, x, grad_middle, vectors, ns, nc):
    main, features = dw.shape[1:]
    rows = main + extra.shape[1]
    micros, half, _ = grad_middle.shape
    size, part = rows // nc, features // ns
    return pl.pallas_call(
        functools.partial(last_kernel, ns=ns, nc=nc),
        in_specs=[pl.BlockSpec(memory_space=pltpu.VMEM)] * 7,
        out_specs=[pl.BlockSpec(memory_space=pltpu.VMEM)] * 2,
        out_shape=[
            jax.ShapeDtypeStruct((micros, 2, half, features), BF16),
            jax.ShapeDtypeStruct((nc, size, part), BF16),
        ],
        scratch_shapes=[
            pltpu.VMEM((rows, features), BF16), pltpu.VMEM((rows, features), BF16), pltpu.VMEM((nc, size, features), BF16),
            pltpu.VMEM((ns, size, part), BF16), pltpu.VMEM((ns, size, part), BF16),
            *axis_sems(2, nc, ns, nc, micros),
        ],
        compiler_params=params(collective_id=5, has_side_effects=True),
        name="last_sums",
    )(dw, extra, *dn, x, grad_middle, vectors)


def pad_rows(rows, multiple):
    extra = -rows.shape[0] % multiple
    return jnp.concatenate([rows, jnp.zeros((extra,) + rows.shape[1:], rows.dtype)]) if extra else rows


def body(
    tokens, cotangent, w_query, w_key, w_value, w_out, w_up, w_down,
    b_query, b_value, b_up, b_out, b_down, gain_attn, shift_attn, gain_ffn, shift_ffn,
):
    ns, nc = lax.axis_size("shard"), lax.axis_size("ctx")
    t = lax.axis_index("tp")
    micros, _, length, features = tokens.shape
    half = length // 2
    heads, head_part = b_query.shape
    head_width = head_part * ns
    up_part = b_up.shape[1]
    feature_part = b_out.shape[0]

    smalls = [b_query, b_value, b_up, b_out, b_down, gain_attn, shift_attn, gain_ffn, shift_ffn]
    flat = jnp.concatenate([v.reshape(-1) for v in smalls])
    small = jnp.pad(flat, (0, -flat.shape[0] % 2048)).reshape(-1, 128)
    w_all, small_all, x_first = gather_first((w_query, w_key, w_value), small, tokens, ns, nc)
    small_all = small_all.reshape(2, ns, -1)
    bias_size, up_size = b_query.size, b_up.size
    biases = small_all[:, :, : 2 * bias_size].reshape(2, ns, 2, heads, head_part)
    biases = biases.transpose(2, 0, 3, 1, 4).reshape(2, 2 * heads * head_width).astype(F32)
    bup = small_all[:, :, 2 * bias_size : 2 * bias_size + up_size].reshape(2, ns, heads, up_part)
    bup = bup.transpose(0, 2, 1, 3).reshape(2, 1, heads * up_part * ns).astype(F32)
    at = 2 * bias_size + up_size
    vectors = small_all[0, :, at : at + 6 * feature_part].reshape(ns, 6, feature_part)
    vectors = vectors.transpose(1, 0, 2).reshape(6, features).astype(F32)
    keys = 2 * nc * half
    aligned = feature_part % 128 == 0
    column_place = place_columns if aligned else place_slot

    def column_shape(w):
        return (2, w.shape[0], features) if aligned else (2, ns) + w.shape

    def whole_columns(w):
        if not aligned:
            w = w.transpose(0, 2, 1, 3).reshape(2, w.shape[2], features)
        return w

    plans = [
        (("ctx", nc, place_distance, True), ("shard", ns, place_rows, False), ("shard", ns, column_place, False)),
        (("shard", ns, column_place, False),),
    ]
    sources = [(tokens, w_up, w_out), (w_down,)]
    specs = [
        [once((1, 1, length, features), (1, 0, 0, 0)), once(w_up.shape), once(w_out.shape)],
        [once(w_down.shape)],
    ]
    shapes = [
        ((nc, 2, half, features), (2, features, w_up.shape[1]), column_shape(w_out)),
        (column_shape(w_down),),
    ]
    x_alls = [x_first.reshape(keys, features), None]
    saved = []
    arrived = []
    for micro in range(micros):
        normed, k, v, q = front(x_alls[micro], w_all, vectors, biases, head_width, half)
        mixed, qx, *more = attend_forward(
            q, k, v, head_width, plans[micro], sources[micro], specs[micro], shapes[micro], micro + 1
        )
        if micro == 0:
            x_alls[1] = more.pop(0).reshape(keys, features)
        arrived += more
        saved.append((normed, k, v, qx, mixed))
    wu, wo, wd = arrived[0], whole_columns(arrived[1]), whole_columns(arrived[2])

    out, grad_middle, grad_mixed, dw, dup, dvec = feed_forward(
        tokens, [entry[4] for entry in saved], cotangent, wo, wu, wd, bup, vectors, jnp.full((1,), t, jnp.int32)
    )

    def spread(v, part):
        return v.reshape(heads, ns, part).transpose(1, 0, 2).reshape(ns, -1)

    def as_rows(v):
        count = v.shape[1] // feature_part
        return v.reshape(ns, count, feature_part).transpose(1, 0, 2).reshape(count, features)

    extra = jnp.stack(
        [pad_rows(jnp.concatenate([dvec[:4], as_rows(spread(dup[part, 0], up_part))]), 16 * nc) for part in range(2)]
    ).astype(BF16)

    width = heads * head_width
    *starts, dn_first, dw_parts, output = attend_back_rows(
        saved[0], grad_mixed, x_alls[0], w_all, head_width, dw, extra, out.reshape(micros, half, features), ns, nc
    )
    dw_now, db_now, sums, dn_second, dw_done = attend_back_shards(
        saved[1], grad_mixed, x_alls[1], w_all, head_width, starts, dw_parts, ns, nc
    )

    db_now = db_now[:, :2].reshape(2, -1, 2, 2 * head_width).transpose(0, 2, 1, 3).reshape(2, 2, width)
    extras = []
    for part in range(2):
        biases = jnp.concatenate([spread(db_now[part, 0], head_part), spread(db_now[part, 1], head_part)], axis=1)
        extras.append(pad_rows(jnp.concatenate([sums[:2], as_rows(biases)]), 16 * nc))
    grad_tokens, attn_done = last_sums(
        dw_now.reshape(2, 3 * width, features), jnp.stack(extras).astype(BF16),
        (dn_first, dn_second), tokens, grad_middle.reshape(micros, half, features), vectors, ns, nc,
    )

    output = output.reshape(micros, 1, length, features)
    grad_tokens = grad_tokens.reshape(micros, 1, length, features)
    done_ffn = dw_done.reshape(-1, feature_part).astype(F32)
    done_attn = attn_done.reshape(-1, feature_part).astype(F32)
    hidden = heads * up_part * ns
    g_out, g_down, g_up = done_ffn[:width], done_ffn[width : width + hidden], done_ffn[width + hidden : width + 2 * hidden]
    tail = done_ffn[width + 2 * hidden :]
    by_kind = done_attn[: 3 * width].reshape(-1, 3, 2 * head_width, feature_part)
    g_query, g_key, g_value = (by_kind[:, i].reshape(width, feature_part).T for i in range(3))
    tail_attn = done_attn[3 * width :]
    g_bup = tail[4:].reshape(-1)[: heads * up_part].reshape(heads, up_part)
    g_heads = tail_attn[2:].reshape(-1)
    g_bq = g_heads[: heads * head_part].reshape(heads, head_part)
    g_bv = g_heads[heads * head_part : 2 * heads * head_part].reshape(heads, head_part)
    return (
        output, grad_tokens, g_query, g_key, g_value, g_out, g_up.T, g_down, g_bq, g_bv, g_bup,
        tail[0], tail[1], tail_attn[0], tail_attn[1], tail[2], tail[3],
    )


def solution(mesh):
    wide, tall = P("shard", "tp"), P("tp", "shard")
    rows, vector = P(None, "shard", "ctx", None), P("shard")
    weights = (wide, wide, wide, tall, wide, tall)
    return jax.shard_map(
        body,
        mesh=mesh,
        in_specs=(rows, rows) + weights + (tall,) * 3 + (vector,) * 6,
        out_specs=(rows, rows) + weights + (tall,) * 3 + (vector,) * 6,
        check_vma=False,
    )
```

profile of v0, /device:TPU:0, one launch (start us, length us, event | category | flops | bytes accessed | tf_op | source)
XLA Modules:
  0.0 360.8 jit_solution(13717516246808196327)
XLA Ops:
  0.7 0.8 reshape.151
  1.4 0.8 reshape.152
  2.2 0.8 reshape.153
  2.9 4.1 %concatenate.27 = bf16[1152]{0:T(1024)(128)(2,1)S(1)} concatenate(bf16[64]{0:T(256)(128)(2,1)S(1)} %reshape.151, bf16[64]{0:T(256)(128)(2,1)S(1)} %reshape.152, bf16[256]{0:T(256)(128)(2,1)S(1)} %reshape.153, bf16[128]{0:T(256)(128)(2,1)} %param.28, bf16[128]{0:T(256)(128)(2,1)} %param.29, bf16[128]{0:T(256)(128)(2,1)} %param.30, bf16[128]{0:T(256)(128)(2,1)} %param.31, ...), dimensions={0} | concatenate | bytes 4608 | tf_op jit(solution)/shard_map/concatenate | solution.py:1040
  7.6 34.5 %gather_first.1 = (bf16[2,3,512,256]{3,2,1,0:T(8,128)(2,1)}, bf16[2,4,16,128]{3,2,1,0:T(8,128)(2,1)}, bf16[4,2,512,512]{3,2,1,0:T(8,128)(2,1)}) custom-call(bf16[128,256]{1,0:T(8,128)(2,1)} %wq_ref.1, bf16[128,256]{1,0:T(8,128)(2,1)} %wk_ref.1, bf16[128,256]{1,0:T(8,128)(2,1)} %wv_ref.1, bf16[16,128]{1,0:T(8,128)(2,1)} %pad_bitcast_fusion.small_ref, ...), custom_call_target="tpu_custom_call" | custom-call | tf_op jit(solution)/shard_map/gather_first/pallas_call | solution.py:151
  42.1 0.8 reshape.156
  43.7 0.7 reshape.174.bias_ref
  44.4 10.8 %front.2 = (bf16[4096,512]{1,0:T(8,128)(2,1)}, bf16[4096,512]{1,0:T(8,128)(2,1)}, bf16[4096,512]{1,0:T(8,128)(2,1)}, bf16[512,512]{1,0:T(8,128)(2,1)}) custom-call(bf16[4096,512]{1,0:T(8,128)(2,1)} %bitcast.113, bf16[2,3,512,256]{3,2,1,0:T(8,128)(2,1)} %get-tuple-element.56.w_ref.refs_7_, f32[6,512]{1,0:T(8,128)} %bitcast.99, f32[2,512]{1,0:T(2,128)} %reshape.174.bias_ref), custom_call_target="tpu_custom_call" | custom-call | flops 4294967296 | bytes 16777216 | tf_op jit(solution)/shard_map/front/pallas_call | solution.py:195
  55.1 38.6 %attend_forward.2 = (bf16[512,512]{1,0:T(8,128)(2,1)}, bf16[512,1024]{1,0:T(8,128)(2,1)}, bf16[4,2,512,512]{3,2,1,0:T(8,128)(2,1)}, bf16[2,512,1024]{2,1,0:T(8,128)(2,1)}, bf16[2,256,512]{2,1,0:T(8,128)(2,1)}) custom-call(bf16[512,512]{1,0:T(8,128)(2,1)} %get-tuple-element.58.refs_0_, bf16[4096,512]{1,0:T(8,128)(2,1)} %get-tuple-element.59.refs_1_, ...), custom_call_target="tpu_custom_call" | custom-call | flops 12884901888 | bytes 8388608 | tf_op jit(solution)/shard_map/attend_forward/pallas_call | solution.py:406
  93.7 10.8 %front.3 = (bf16[4096,512]{1,0:T(8,128)(2,1)}, bf16[4096,512]{1,0:T(8,128)(2,1)}, bf16[4096,512]{1,0:T(8,128)(2,1)}, bf16[512,512]{1,0:T(8,128)(2,1)}) custom-call(bf16[4096,512]{1,0:T(8,128)(2,1)} %bitcast.115, bf16[2,3,512,256]{3,2,1,0:T(8,128)(2,1)} %get-tuple-element.56.w_ref.refs_7_, f32[6,512]{1,0:T(8,128)} %bitcast.100, f32[2,512]{1,0:T(2,128)} %reshape.174.bias_ref), custom_call_target="tpu_custom_call" | custom-call | flops 4294967296 | bytes 16777216 | tf_op jit(solution)/shard_map/front/pallas_call | solution.py:195
  104.5 30.8 %attend_forward.3 = (bf16[512,512]{1,0:T(8,128)(2,1)}, bf16[512,1024]{1,0:T(8,128)(2,1)}, bf16[2,1024,512]{2,1,0:T(8,128)(2,1)}) custom-call(bf16[512,512]{1,0:T(8,128)(2,1)} %get-tuple-element.64.refs_0_, bf16[4096,512]{1,0:T(8,128)(2,1)} %get-tuple-element.65.refs_1_, bf16[4096,512]{1,0:T(8,128)(2,1)} %get-tuple-element.66.refs_2_, bf16[1024,128]{1,0:T(8,128)(2,1)} %refs_3_.3), custom_call_target="tpu_custom_call" | custom-call | flops 12884901888 | bytes 8388608 | tf_op jit(solution)/shard_map/attend_forward/pallas_call | solution.py:406
  135.4 0.7 reshape.175.bup_ref
  136.1 25.6 %feed_forward.1 = (bf16[1024,512]{1,0:T(8,128)(2,1)}, f32[1024,512]{1,0:T(8,128)}, bf16[1024,512]{1,0:T(8,128)(2,1)}, bf16[2,2304,512]{2,1,0:T(8,128)(2,1)}, f32[2,1,1024]{2,1,0:T(1,128)}, /*index=5*/f32[8,512]{1,0:T(8,128)}) custom-call(s32[1]{0:T(128)} %bitcast.5.where_ref, bf16[2,1,1024,512]{3,2,1,0:T(8,128)(2,1)} %x_ref.3, ...), custom_call_target="tpu_custom_call" | custom-call | flops 14495514624 | bytes 23592960 | tf_op jit(solution)/shard_map/feed_forward/pallas_call | solution.py:918
  161.7 0.7 convert.78
  162.8 0.7 slice.187
  163.7 0.7 pad_maximum_fusion.refs_10_
  164.4 75.3 %attend_back.2 = (f32[4,3,128,512]{3,2,1,0:T(8,128)}, f32[4,8,128]{2,1,0:T(8,128)}, f32[8,512]{1,0:T(8,128)}, f32[512,512]{1,0:T(8,128)}, bf16[4,592,128]{2,1,0:...) custom-call(bf16[512,1024]{1,0:T(8,128)(2,1)} %get-tuple-element.61.refs_0_, bf16[4096,512]{1,0:T(8,128)(2,1)} %get-tuple-element.59.refs_1_, ...), custom_call_target="tpu_custom_call" | custom-call | flops 32212254720 | bytes 16777216 | tf_op jit(solution)/shard_map/attend_back/pallas_call | solution.py:776
  239.6 73.3 %attend_back.3 = (bf16[4,3,128,512]{3,2,1,0:T(8,128)(2,1)}, f32[4,8,128]{2,1,0:T(8,128)}, f32[8,512]{1,0:T(8,128)}, f32[512,512]{1,0:T(8,128)}, bf16[4,592,128]{2,1,0:T(8,128)(2,1)}) custom-call(bf16[512,1024]{1,0:T(8,128)(2,1)} %get-tuple-element.78.refs_0_, bf16[4096,512]{1,0:T(8,128)(2,1)} %get-tuple-element.65.refs_1_, ...), custom_call_target="tpu_custom_call" | custom-call | flops 32212254720 | bytes 16777216 | tf_op jit(solution)/shard_map/attend_back/pallas_call | solution.py:776
  312.9 0.7 slice.188
  314.6 0.7 slice.189
  315.5 0.7 pad_maximum_fusion.1.extra_ref
  316.2 31.3 %last_sums.1 = (bf16[2,2,512,512]{3,2,1,0:T(8,128)(2,1)}, bf16[4,208,128]{2,1,0:T(8,128)(2,1)}) custom-call(bf16[2,768,512]{2,1,0:T(8,128)(2,1)} %bitcast.91, bf16[2,64,512]{2,1,0:T(8,128)(2,1)} %pad_maximum_fusion.1.extra_ref, f32[512,512]{1,0:T(8,128)} %get-tuple-element.87.dn0_ref, f32[512,512]{1,0:T(8,128)} %get-tuple-element.88.dn1_ref, ...), custom_call_target="tpu_custom_call" | custom-call | tf_op jit(solution)/shard_map/last_sums/pallas_call | solution.py:1003
  347.5 1.0 bitcast_convert_fusion.1
  348.6 0.8 copy.68
  349.3 0.8 copy.69
  350.1 0.8 copy.70
  352.2 1.0 fusion.8
  353.3 2.0 copy.64
  355.3 0.7 slice.155
  357.2 1.3 copy.81
  358.5 1.0 copy-done.1
  359.5 1.3 copy.82
  (53 shorter events, 5.7 us)
Async XLA Ops:
  347.5 4.6 %copy-start.2 = (bf16[4,592,128]{2,1,0:T(8,128)(2,1)S(1)}, bf16[4,592,128]{2,1,0:T(8,128)(2,1)}, u32[]{:S(2)}) copy-start(bf16[4,592,128]{2,1,0:T(8,128)(2,1)} %get-tuple-element.92) | copy-start | bytes 1818628
  352.2 4.9 %copy-start = (bf16[2,2,512,512]{3,2,1,0:T(8,128)(2,1)S(1)}, bf16[2,2,512,512]{3,2,1,0:T(8,128)(2,1)}, u32[]{:S(2)}) copy-start(bf16[2,2,512,512]{3,2,1,0:T(8,128)(2,1)} %get-tuple-element.77) | copy-start | bytes 6291460
  357.2 2.3 copy-start.1
where the time goes:
time: 362 us; the launch traced here: 361 us
  Pallas kernels  331 us (91%)
  local copies, waits for them, and re-layouts  25.5 us (7%)
    pallas_call x2, Pallas kernels, attend_back(): pl.pallas_call(functools.partial(attend_back_kernel, width=width, nc=nc,...  149 us
    pallas_call x2, Pallas kernels, attend_forward(): pl.pallas_call(functools.partial(attend_kernel, kc=kc, width=width, plans...  69.4 us
    pallas_call x1, Pallas kernels, gather_first(): pl.pallas_call(functools.partial(gather_kernel, ns, nc), grid=(1,), in_sp...  34.5 us
    pallas_call x1, Pallas kernels, last_sums(): pl.pallas_call(functools.partial(last_kernel, ns=ns, nc=nc), in_specs=[pl...  31.3 us
    pallas_call x1, Pallas kernels, feed_forward(): pl.pallas_call(ffn_kernel, grid_spec=pltpu.PrefetchScalarGridSpec(num_sca...  25.6 us
    pallas_call x2, Pallas kernels, front(): pl.pallas_call(functools.partial(front_kernel, q_scale=LOG2E / math.sqrt(...  21.6 us

commit v1 on v0

--- a/solution.py
+++ b/solution.py
@@ -68,7 +68,97 @@
     )
 
 
-def gather_kernel(ns, nc, wq_ref, wk_ref, wv_ref, small_ref, x_block, w_out, small_out, x_out, *sems):
+def greet_first(counts):
+    barrier = pltpu.get_barrier_semaphore()
+    for name, count in counts:
+        me = lax.axis_index(name)
+        for d in range(1, count):
+            pl.semaphore_signal(barrier, inc=1, device_id={name: me ^ d}, device_id_type=MESH)
+
+
+def greet_wait(counts):
+    pl.semaphore_wait(pltpu.get_barrier_semaphore(), sum(count - 1 for _, count in counts))
+
+
+def greet(counts):
+    greet_first(counts)
+    greet_wait(counts)
+
+
+class Gather:
+
+    def __init__(self, name, count, source, theirs, target, place, sems):
+        self.name, self.count, self.source, self.theirs = name, count, source, theirs
+        self.target, self.place = target, place
+        self.out_sem, self.in_sem, self.cross_out, self.cross_in, self.local = sems
+        self.me = lax.axis_index(name)
+
+    def first(self, d):
+        where = {self.name: self.me ^ d}
+        return send(self.source, self.place(self.target, 0, self.me, d), self.out_sem.at[d], self.in_sem.at[d], where)
+
+    def cross(self, d):
+        where = {"tp": 1 - lax.axis_index("tp")}
+        owner = self.me ^ d
+        source = self.place(self.target, 0, owner, d) if d else self.source
+        return send(source, self.place(self.target, 1, owner, d), self.cross_out.at[d], self.cross_in.at[d], where)
+
+    def locals(self):
+        copies = [pltpu.make_async_copy(self.source, self.place(self.target, 0, self.me, 0), self.local.at[0])]
+        if self.theirs is not None:
+            copies.append(pltpu.make_async_copy(self.theirs, self.place(self.target, 1, self.me, 0), self.local.at[1]))
+        return copies
+
+    def crossed(self):
+        return range(0 if self.theirs is None else 1, self.count)
+
+    def start(self, late=0):
+        for d in range(1, self.count - late):
+            self.first(d).start()
+        for copy in self.locals():
+            copy.start()
+        if self.theirs is None:
+            self.cross(0).start()
+
+    def forward(self, distances=None):
+        for d in distances or range(1, self.count):
+            self.first(d).wait_recv()
+            self.cross(d).start()
+
+    def finish(self):
+        for d in range(1, self.count):
+            self.first(d).wait_send()
+        for d in self.crossed():
+            self.cross(d).wait()
+        for copy in self.locals():
+            copy.wait()
+
+
+def place_rows(ref, part, owner, d):
+    size = ref.shape[1] // lax.axis_size("shard")
+    return ref.at[part, pl.ds(pl.multiple_of(owner * size, size), size), :]
+
+
+def place_columns(ref, part, owner, d):
+    size = ref.shape[2] // lax.axis_size("shard")
+    return ref.at[part, :, pl.ds(pl.multiple_of(owner * size, size), size)]
+
+
+def place_slot(ref, part, owner, d):
+    return ref.at[part, owner]
+
+
+def place_distance(ref, part, owner, d):
+    return ref.at[d, part]
+
+
+def gather_sems(count):
+    dma = pltpu.SemaphoreType.DMA
+    return [dma((count,)), dma((count,)), dma((count,)), dma((count,)), dma((2,))]
+
+
+def gather_kernel(ns, nc, wq_ref, wk_ref, wv_ref, x_block, *refs):
+    tables, (w_out, small_out, x_out, small_ref), sems = refs[:-17], refs[-17:-13], refs[-13:]
     w_send, w_recv, s_send, s_recv, x_send, x_recv, wt_send, wt_recv, st_send, st_recv, xt_send, xt_recv, local = sems
     w_refs = (wq_ref, wk_ref, wv_ref)
     kinds = range(3)
@@ -80,13 +170,15 @@
     depth = wq_ref.shape[0]
     half = x_ref.shape[0] // 2
 
-    barrier = pltpu.get_barrier_semaphore()
-    for d in range(1, ns):
-        pl.semaphore_signal(barrier, inc=1, device_id={"shard": s ^ d}, device_id_type=MESH)
-    for d in range(1, nc):
-        pl.semaphore_signal(barrier, inc=1, device_id={"ctx": c ^ d}, device_id_type=MESH)
-    pl.semaphore_signal(barrier, inc=1, device_id={"tp": other}, device_id_type=MESH)
-    pl.semaphore_wait(barrier, ns + nc - 1)
+    peers = [("tp", 2), ("ctx", nc), ("shard", ns)]
+    greet_first(peers)
+    small_ref[...] = jnp.zeros_like(small_ref)
+    row = 0
+    for table in tables:
+        count, lanes = table.shape
+        small_ref[row : row + count, :lanes] = table[...].astype(F32)
+        row += count
+    greet_wait(peers)
 
     def w_rows(part, kind, owner):
         return w_out.at[part, kind, pl.ds(pl.multiple_of(owner * depth, depth), depth), :]
@@ -100,8 +192,21 @@
         return copy
 
     x_copies, w_copies, s_copies = {}, {}, {}
-    for d in range(1, nc):
-        x_copies[d] = begin(x_rows(t), x_out.at[d, 0], x_send.at[d], x_recv.at[d], {"ctx": c ^ d})
+    size = half // 2
+
+    def x_part(d, h):
+        return x_out.at[d, 0, pl.ds(h * size, size), :]
+
+    def x_begin(source, d, h, to):
+        copy = begin(source, x_part(d, h), x_send.at[d, h], x_recv.at[d, h], {"ctx": c ^ to})
+        x_copies[d, h] = copy
+
+    relayed = nc == 4
+    for h in range(2):
+        for d in range(1, 3 if relayed else nc):
+            part = h if d % 2 else 1 - h
+            source = x_ref.at[pl.ds(pl.multiple_of(t * half + part * size, size), size), :]
+            x_begin(source, d, part, d)
     for d in range(1, ns):
         for k in kinds:
             w_copies[d, k] = begin(
@@ -118,6 +223,12 @@
     ]
     for copy in locals_:
         copy.start()
+    if relayed:
+        x_copies[1, 0].wait_recv()
+        x_begin(x_part(1, 0), 3, 0, 2)
+        x_copies[2, 1].wait_recv()
+        x_begin(x_part(2, 1), 3, 1, 1)
+    waited = {(1, 0), (2, 1)} if relayed else set()
     for d in range(1, max(ns, nc)):
         if d < ns:
             for k in kinds:
@@ -132,7 +243,9 @@
                 begin(small_out.at[0, s ^ d], small_out.at[1, s ^ d], st_send.at[d], st_recv.at[d], {"tp": other})
             )
         if d < nc:
-            x_copies[d].wait_recv()
+            for h in range(2):
+                if (d, h) not in waited:
+                    x_copies[d, h].wait_recv()
             last.append(begin(x_out.at[d, 0], x_out.at[d, 1], xt_send.at[d], xt_recv.at[d], {"tp": other}))
     for copies in (x_copies, w_copies, s_copies):
         for copy in copies.values():
@@ -143,36 +256,38 @@
         copy.wait()
 
 
-def gather_first(weights, small, tokens, ns, nc):
+def gather_first(weights, tables, tokens, ns, nc):
     depth, width = weights[0].shape
     length, features = tokens.shape[2:]
+    rows = -(-sum(table.shape[0] for table in tables) // 8) * 8
+    lanes = -(-max(table.shape[1] for table in tables) // 128) * 128
     dma = pltpu.SemaphoreType.DMA
     vmem = pl.BlockSpec(memory_space=pltpu.VMEM)
     return pl.pallas_call(
         functools.partial(gather_kernel, ns, nc),
         grid=(1,),
-        in_specs=[vmem] * 4 + [once((1, 1, length, features))],
+        in_specs=[vmem] * 3 + [once((1, 1, length, features))] + [vmem] * len(tables),
         out_specs=[pl.BlockSpec(memory_space=pl.ANY)] * 3,
         out_shape=[
             jax.ShapeDtypeStruct((2, 3, ns * depth, width), BF16),
-            jax.ShapeDtypeStruct((2, ns) + small.shape, BF16),
+            jax.ShapeDtypeStruct((2, ns, rows, lanes), F32),
             jax.ShapeDtypeStruct((nc, 2, length // 2, features), BF16),
         ],
-        scratch_shapes=[dma((3, ns)), dma((3, ns)), dma((ns,)), dma((ns,)), dma((nc,)), dma((nc,))]
+        scratch_shapes=[pltpu.VMEM((rows, lanes), F32)]
+        + [dma((3, ns)), dma((3, ns)), dma((ns,)), dma((ns,)), dma((nc, 2)), dma((nc, 2))]
         + [dma((3, ns)), dma((3, ns)), dma((ns,)), dma((ns,)), dma((nc,)), dma((nc,)), dma((6,))],
         compiler_params=params(collective_id=0, has_side_effects=True),
         name="gather_first",
-    )(*weights, small, tokens)
-
-
-def front_kernel(x_ref, w_ref, vec_ref, bias_ref, n_ref, k_ref, v_ref, q_ref, *, q_scale):
-    step = pl.program_id(0)
+    )(*weights, tokens, *tables)
+
+
+def project_rows(x, w_ref, vec_ref, bias_ref, n_ref, k_ref, v_ref):
     gain, shift = vec_ref[2:3], vec_ref[3:4]
     width = w_ref.shape[3]
-    size = x_ref.shape[0] // 4
+    size = n_ref.shape[0] // 4
     for i in range(4):
         rows = slice(i * size, (i + 1) * size)
-        unit, _ = unit_norm(x_ref[rows].astype(F32))
+        unit, _ = unit_norm(x(i, size).astype(F32))
         normed = (unit * gain + shift).astype(BF16)
         n_ref[rows] = normed
         for part in range(2):
@@ -180,45 +295,80 @@
             k_ref[rows, cols] = dot_nn(normed, w_ref[part, 1]).astype(BF16)
             v_ref[rows, cols] = (dot_nn(normed, w_ref[part, 2]) + bias_ref[1:2, cols]).astype(BF16)
 
+
+def project_query(w_ref, bias_ref, n_ref, q_ref, q_scale):
+    width = w_ref.shape[3]
+    normed = n_ref[: q_ref.shape[0]]
+    for part in range(2):
+        cols = slice(part * width, (part + 1) * width)
+        q_ref[:, cols] = ((dot_nn(normed, w_ref[part, 0]) + bias_ref[0:1, cols]) * q_scale).astype(BF16)
+
+
+def front_kernel(
+    x_ref, w_ref, vec_ref, bias_ref, guest_ref, n_ref, k_ref, v_ref, q_ref, guest_all, *sems, q_scale, ns, place, size
+):
+    step = pl.program_id(0)
+    gather = Gather("shard", ns, guest_ref.at[pl.ds(0, size), :], None, guest_all, place, sems)
+
+    peers = [("tp", 2), ("shard", ns)]
+
     @pl.when(step == 0)
     def _():
-        normed = n_ref[: q_ref.shape[0]]
-        for part in range(2):
-            cols = slice(part * width, (part + 1) * width)
-            q_ref[:, cols] = ((dot_nn(normed, w_ref[part, 0]) + bias_ref[0:1, cols]) * q_scale).astype(BF16)
-
-
-def front(x_all, weights, vectors, biases, head_width, half):
+        greet_first(peers)
+
+    @pl.when(step == 1)
+    def _():
+        greet_wait(peers)
+        gather.start()
+
+    project_rows(lambda i, size: x_ref[i * size : (i + 1) * size], w_ref, vec_ref, bias_ref, n_ref, k_ref, v_ref)
+
+    @pl.when(step == 0)
+    def _():
+        project_query(w_ref, bias_ref, n_ref, q_ref, q_scale)
+
+    @pl.when(step == pl.num_programs(0) - 1)
+    def _():
+        gather.forward()
+        gather.finish()
+
+
+def front(x_all, weights, vectors, biases, head_width, half, guest, guest_rows, guest_shape, ns, place, number):
     keys, features = x_all.shape
     block = 2 * half
     width = 2 * weights.shape[3]
+    scale = LOG2E / math.sqrt(head_width)
     return pl.pallas_call(
-        functools.partial(front_kernel, q_scale=LOG2E / math.sqrt(head_width)),
+        functools.partial(front_kernel, q_scale=scale, ns=ns, place=place, size=guest_rows),
         grid=(keys // block,),
         in_specs=[
             pl.BlockSpec((block, features), lambda i: (i, 0)),
             once(weights.shape),
             once(vectors.shape),
             once(biases.shape),
+            once(guest.shape),
         ],
         out_specs=[
             pl.BlockSpec((block, features), lambda i: (i, 0)),
             pl.BlockSpec((block, width), lambda i: (i, 0)),
             pl.BlockSpec((block, width), lambda i: (i, 0)),
             full_spec((half, width)),
+            pl.BlockSpec(memory_space=pl.ANY),
         ],
         out_shape=[
             jax.ShapeDtypeStruct((keys, features), BF16),
             jax.ShapeDtypeStruct((keys, width), BF16),
             jax.ShapeDtypeStruct((keys, width), BF16),
             jax.ShapeDtypeStruct((half, width), BF16),
+            jax.ShapeDtypeStruct(guest_shape, BF16),
         ],
-        compiler_params=params(),
+        scratch_shapes=gather_sems(ns),
+        compiler_params=params(collective_id=number, has_side_effects=True),
         cost_estimate=pl.CostEstimate(
             flops=4 * keys * features * width, bytes_accessed=8 * keys * features, transcendentals=keys
         ),
         name="front",
-    )(x_all, weights, vectors, biases)
+    )(x_all, weights, vectors, biases, guest)
 
 
 def with_parts(lane, base, values, first, width):
@@ -231,89 +381,6 @@
     )
     inside = (lane < width) if first else (lane >= width)
     return jnp.where(inside, base, extra)
-
-
-def greet(counts):
-    barrier = pltpu.get_barrier_semaphore()
-    total = 0
-    for name, count in counts:
-        me = lax.axis_index(name)
-        for d in range(1, count):
-            pl.semaphore_signal(barrier, inc=1, device_id={name: me ^ d}, device_id_type=MESH)
-            total += 1
-    pl.semaphore_wait(barrier, total)
-
-
-class Gather:
-
-    def __init__(self, name, count, source, theirs, target, place, sems):
-        self.name, self.count, self.source, self.theirs = name, count, source, theirs
-        self.target, self.place = target, place
-        self.out_sem, self.in_sem, self.cross_out, self.cross_in, self.local = sems
-        self.me = lax.axis_index(name)
-
-    def first(self, d):
-        where = {self.name: self.me ^ d}
-        return send(self.source, self.place(self.target, 0, self.me, d), self.out_sem.at[d], self.in_sem.at[d], where)
-
-    def cross(self, d):
-        where = {"tp": 1 - lax.axis_index("tp")}
-        owner = self.me ^ d
-        source = self.place(self.target, 0, owner, d) if d else self.source
-        return send(source, self.place(self.target, 1, owner, d), self.cross_out.at[d], self.cross_in.at[d], where)
-
-    def locals(self):
-        copies = [pltpu.make_async_copy(self.source, self.place(self.target, 0, self.me, 0), self.local.at[0])]
-        if self.theirs is not None:
-            copies.append(pltpu.make_async_copy(self.theirs, self.place(self.target, 1, self.me, 0), self.local.at[1]))
-        return copies
-
-    def crossed(self):
-        return range(0 if self.theirs is None else 1, self.count)
-
-    def start(self):
-        for d in range(1, self.count):
-            self.first(d).start()
-        for copy in self.locals():
-            copy.start()
-        if self.theirs is None:
-            self.cross(0).start()
-
-    def forward(self):
-        for d in range(1, self.count):
-            self.first(d).wait_recv()
-            self.cross(d).start()
-
-    def finish(self):
-        for d in range(1, self.count):
-            self.first(d).wait_send()
-        for d in self.crossed():
-            self.cross(d).wait()
-        for copy in self.locals():
-            copy.wait()
-
-
-def place_rows(ref, part, owner, d):
-    size = ref.shape[1] // lax.axis_size("shard")
-    return ref.at[part, pl.ds(pl.multiple_of(owner * size, size), size), :]
-
-
-def place_columns(ref, part, owner, d):
-    size = ref.shape[2] // lax.axis_size("shard")
-    return ref.at[part, :, pl.ds(pl.multiple_of(owner * size, size), size)]
-
-
-def place_slot(ref, part, owner, d):
-    return ref.at[part, owner]
-
-
-def place_distance(ref, part, owner, d):
-    return ref.at[d, part]
-
-
-def gather_sems(count):
-    dma = pltpu.SemaphoreType.DMA
-    return [dma((count,)), dma((count,)), dma((count,)), dma((count,)), dma((2,))]
 
 
 def attend_kernel(*refs, kc, width, plans):
@@ -330,7 +397,7 @@
 
     def gathers(wanted):
         found = []
-        for i, (name, number, place, split) in enumerate(plans):
+        for i, (name, number, place, split, start) in enumerate(plans):
             if name != wanted:
                 continue
             source, theirs = sources[i], None
@@ -339,22 +406,20 @@
                 half = source.shape[0] // 2
                 theirs = source.at[pl.ds(pl.multiple_of((1 - t) * half, half), half), :]
                 source = source.at[pl.ds(pl.multiple_of(t * half, half), half), :]
+            elif start:
+                source = source.at[pl.ds(start, source.shape[0] - start), :]
             found.append(Gather(name, number, source, theirs, targets[i], place, sems[5 * i : 5 * i + 5]))
         return found
 
-    counts = {name: number for name, number, _, _ in plans}
+    counts = {name: number for name, number, *_ in plans}
+
+    peers = [("tp", 2)] + list(counts.items())
+    far = counts.get("ctx", 1) - 1
 
     @pl.when(step == 0)
     def _():
-        greet([("tp", 2)] + list(counts.items()))
-        for name in counts:
-            for gather in gathers(name):
-                gather.start()
-
-    @pl.when(step == last)
-    def _():
-        for gather in gathers("ctx"):
-            gather.forward()
+        greet_first(peers)
+
 
     rows, lanes = q_ref.shape
     keys = k_ref.shape[0]
@@ -372,6 +437,27 @@
             here = jnp.max(part.reshape(kc // 8, 8, rows), axis=0)
             top = here if top is None else jnp.maximum(top, here)
         tops.append(jnp.max(top, axis=0, keepdims=True))
+
+    @pl.when(step == 0)
+    def _():
+        greet_wait(peers)
+        for gather in gathers("shard"):
+            gather.start()
+        for gather in gathers("ctx"):
+            gather.start(1)
+
+    @pl.when(step == 2)
+    def _():
+        for gather in gathers("ctx"):
+            gather.first(far).start()
+            gather.forward(range(1, far))
+
+    @pl.when(step == last)
+    def _():
+        for gather in gathers("shard"):
+            if not far:
+                gather.forward()
+
     outs = []
     for h in range(2):
         inside_v = (lane_v < width) if h == 0 else (lane_v >= width)
@@ -390,8 +476,11 @@
 
     @pl.when(step == last)
     def _():
-        for gather in gathers("shard"):
-            gather.forward()
+        if far:
+            for gather in gathers("shard"):
+                gather.forward()
+            for gather in gathers("ctx"):
+                gather.forward([far])
         for name in counts:
             for gather in gathers(name):
                 gather.finish()
@@ -560,14 +649,13 @@
     def spread_one(self, d):
         self.crossing(d).wait()
         sum_rows(self.total.at[d], 0, self.dn_own(d), 0, self.received.at[d], 0, self.received.shape[1])
-        if d:
-            self.ctx.copy(d, self.source, self.target).start()
+        self.ctx.copy(d, self.source, self.target).start()
 
     def finish(self):
         self.ctx.wait(self.source, self.target)
 
-    def rows(self, at, size):
-        value = self.total[0, pl.ds(at, size), :].astype(F32)
+    def rows(self, own, at, size):
+        value = own[pl.ds(at, size), :]
         for d in range(1, self.ctx.count):
             value += self.blocks[d, pl.ds(at, size), :].astype(F32)
         return value
@@ -650,7 +738,7 @@
     starts = refs[at : at + 3] if started else ()
     at += 3 if started else 0
     extra_in, at = refs[at : at + n_in], at + n_in
-    (dw_ref, db_ref, sums_ref, dn_done), at = refs[at : at + 4], at + 4
+    (dw_ref, db_ref, sums_ref, dn_done, dn_other), at = refs[at : at + 5], at + 5
     extra_out, at = refs[at : at + n_out], at + n_out
     gx_all, dq_acc, dn_acc, dw_acc, dn_sent, dn_received, dn_total, dn_blocks, tp_out, tp_in, ctx_out, ctx_in = refs[at : at + 12]
     extra_scratch = refs[at + 12 :]
@@ -662,7 +750,11 @@
 
     @pl.when((i == 0) & (j == 0))
     def _():
-        greet(guest.peers)
+        greet_first(guest.peers)
+
+    @pl.when((i == 0) & (j == 1))
+    def _():
+        greet_wait(guest.peers)
         guest.begin()
 
     @pl.when((i == 1) & (j == 0))
@@ -675,7 +767,7 @@
         def _(d=d):
             inputs.crossing(d).start()
 
-        @pl.when((i == nc - d) & (j == last_pair - 1))
+        @pl.when((i == nc - d) & (j == 1))
         def _(d=d):
             inputs.spread_one(d)
 
@@ -683,27 +775,27 @@
         base, (gx_all, dq_acc, dn_acc, dw_acc, db_ref, sums_ref), starts, width
     )
 
-    @pl.when(j == last_pair)
-    def _():
-        half = dn_acc.shape[0] // 2
+    half = dn_acc.shape[0] // 2
+
+    @pl.when((j == last_pair) & (i < nc - 1))
+    def _():
         for part in range(2):
             dn_sent[nc - 1 - i, part] = dn_acc[part * half : (part + 1) * half].astype(BF16)
 
     @pl.when((i == nc - 1) & (j == last_pair))
     def _():
         dw_ref[...] = dw_acc[...].astype(dw_ref.dtype)
-        inputs.crossing(0).start()
+        dn_other[...] = dn_acc[half:].astype(BF16)
         guest.end()
-        inputs.spread_one(0)
         inputs.finish()
         size = 64
 
         def one(r, carry):
             here = pl.multiple_of(r * size, size)
-            dn_done[pl.ds(here, size), :] = inputs.rows(here, size)
+            dn_done[pl.ds(here, size), :] = inputs.rows(dn_acc, here, size)
             return carry
 
-        lax.fori_loop(0, dn_done.shape[0] // size, one, 0)
+        lax.fori_loop(0, half // size, one, 0)
 
 
 class HostRows:
@@ -789,15 +881,17 @@
             key_block((size, features), False),
             pl.BlockSpec((1, 3, features, lanes), lambda i, j: (j // each, 0, 0, j % each)),
         ]
-        + [once(start.shape) for start in starts]
+        + [once(value.shape) for value in starts]
         + in_specs,
-        out_specs=[full_spec(stack), full_spec((pairs, 8, lanes)), full_spec((8, features)), full_spec((rows, features))]
+        out_specs=[full_spec(stack), full_spec((pairs, 8, lanes)), full_spec((8, features))]
+        + [full_spec((rows, features))] * 2
         + out_specs,
         out_shape=[
             jax.ShapeDtypeStruct(stack, kind),
             jax.ShapeDtypeStruct((pairs, 8, lanes), F32),
             jax.ShapeDtypeStruct((8, features), F32),
             jax.ShapeDtypeStruct((rows, features), F32),
+            jax.ShapeDtypeStruct((rows, features), BF16),
         ]
         + outs,
         scratch_shapes=[
@@ -851,8 +945,8 @@
 
 
 def ffn_kernel(
-    where_ref, x_ref, o0_ref, o1_ref, g_ref, w_out, w_up, w_down, bup_ref, vec_ref,
-    out_ref, gm_ref, gx_ref, dw_ref, dup_ref, dvec_ref, dw_acc,
+    where_ref, x_ref, o0_ref, o1_ref, g_ref, w_out, w_up, down_first, down_rest, bup_ref, vec_ref,
+    out_ref, gm_ref, gx_ref, dw_ref, dup_ref, dvec_ref, dw_acc, w_down,
 ):
     step = pl.program_id(0)
     steps = pl.num_programs(0)
@@ -862,6 +956,9 @@
 
     @pl.when(step == 0)
     def _():
+        split = down_first.shape[1]
+        w_down[:, :split] = down_first[...]
+        w_down[:, split:] = down_rest[...]
         dw_acc[...] = jnp.zeros_like(dw_acc)
         dup_ref[...] = jnp.zeros_like(dup_ref)
         dvec_ref[...] = jnp.zeros_like(dvec_ref)
@@ -905,7 +1002,7 @@
         dw_ref[...] = dw_acc[...].astype(BF16)
 
 
-def feed_forward(tokens, mixed, cotangent, w_out, w_up, w_down, b_up, vectors, where):
+def feed_forward(tokens, mixed, cotangent, w_out, w_up, down_first, down_rest, b_up, vectors, where):
     micros, _, length, features = tokens.shape
     block = 256
     half = length // 2
@@ -926,11 +1023,11 @@
                 pl.BlockSpec((block, 2 * hw), lambda i, t: (jnp.maximum(i - each, 0), 0)),
                 input_spec,
             ]
-            + [once(w.shape) for w in (w_out, w_up, w_down)]
+            + [once(w.shape) for w in (w_out, w_up, down_first, down_rest)]
             + [once(b_up.shape), once(vectors.shape)],
             out_specs=[row_spec] * 3
             + [full_spec((2, total, features)), full_spec((2, 1, hidden)), full_spec((8, features))],
-            scratch_shapes=[pltpu.VMEM((2, total, features), F32)],
+            scratch_shapes=[pltpu.VMEM((2, total, features), F32), pltpu.VMEM((2, hidden, features), BF16)],
         ),
         out_shape=[
             jax.ShapeDtypeStruct((rows, features), BF16),
@@ -945,14 +1042,14 @@
             flops=12 * rows * total * features, bytes_accessed=20 * total * features, transcendentals=4 * rows * hidden
         ),
         name="feed_forward",
-    )(where, tokens, *mixed, cotangent, w_out, w_up, w_down, b_up, vectors)
+    )(where, tokens, *mixed, cotangent, w_out, w_up, down_first, down_rest, b_up, vectors)
 
 
 def last_kernel(
-    dw_ref, extra_ref, dn0_ref, dn1_ref, x_ref, gm_ref, vec_ref,
+    dw_ref, extra_ref, dn0_ref, dn1_ref, other0_ref, other1_ref, x_ref, gm_ref, vec_ref,
     grad_ref, blocks_ref,
-    w_received, w_total, w_blocks, z_parts, z_received,
-    wtp_out, wtp_in, wctx_out, wctx_in, z_out, z_in, back_out, back_in, row_out, row_in, *, ns, nc,
+    dn_received, w_received, w_total, w_blocks, z_parts, z_received,
+    dn_out, dn_in, wtp_out, wtp_in, wctx_out, wctx_in, z_out, z_in, back_out, back_in, row_out, row_in, *, ns, nc,
 ):
     t = lax.axis_index("tp")
     half = grad_ref.shape[2]
@@ -967,14 +1064,18 @@
     def row(micro):
         return cross(grad_ref.at[micro, t], grad_ref.at[micro, t], (row_out, row_in), micro)
 
+    others = [cross(ref, dn_received.at[m], (dn_out, dn_in), m) for m, ref in enumerate((other0_ref, other1_ref))]
+
     def finish_rows(micro, dn_ref):
         size = 64
+        others[micro].wait()
 
         def one(i, carry):
             at = pl.multiple_of(i * size, size)
             unit, inverse = unit_norm(x_ref[micro, 0, pl.ds(t * half + at, size), :].astype(F32))
             value = gm_ref[micro, pl.ds(at, size), :] + norm_back(
-                dn_ref[pl.ds(at, size), :], unit, inverse, vec_ref[2:3]
+                dn_ref[pl.ds(at, size), :] + dn_received[micro, pl.ds(at, size), :].astype(F32),
+                unit, inverse, vec_ref[2:3],
             )
             grad_ref[micro, t, pl.ds(at, size), :] = value.astype(BF16)
             return carry
@@ -984,6 +1085,8 @@
 
     greet([("tp", 2), ("ctx", nc), ("shard", ns)])
     rows.start()
+    for copy in others:
+        copy.start()
     rows.spread()
     finish_rows(0, dn0_ref)
     rows.finish(z_parts)
@@ -1002,20 +1105,68 @@
     size, part = rows // nc, features // ns
     return pl.pallas_call(
         functools.partial(last_kernel, ns=ns, nc=nc),
-        in_specs=[pl.BlockSpec(memory_space=pltpu.VMEM)] * 7,
+        in_specs=[pl.BlockSpec(memory_space=pltpu.VMEM)] * 9,
         out_specs=[pl.BlockSpec(memory_space=pltpu.VMEM)] * 2,
         out_shape=[
             jax.ShapeDtypeStruct((micros, 2, half, features), BF16),
             jax.ShapeDtypeStruct((nc, size, part), BF16),
         ],
         scratch_shapes=[
+            pltpu.VMEM((micros, half, features), BF16),
             pltpu.VMEM((rows, features), BF16), pltpu.VMEM((rows, features), BF16), pltpu.VMEM((nc, size, features), BF16),
             pltpu.VMEM((ns, size, part), BF16), pltpu.VMEM((ns, size, part), BF16),
-            *axis_sems(2, nc, ns, nc, micros),
+            *axis_sems(micros, 2, nc, ns, nc, micros),
         ],
         compiler_params=params(collective_id=5, has_side_effects=True),
         name="last_sums",
     )(dw, extra, *dn, x, grad_middle, vectors)
+
+
+def results_kernel(out_ref, grad_ref, ffn_ref, attn_ref, *refs, heads, head_part, up_part):
+    (out, grad_tokens, g_query, g_key, g_value, g_out, g_up, g_down, g_bq, g_bv, g_bup, *vectors) = refs
+    out[...] = out_ref[...]
+    grad_tokens[...] = grad_ref[...]
+    width, lanes = g_out.shape
+    hidden = g_down.shape[0]
+    pair = 2 * width // heads
+
+    def values(ref, at, size):
+        return ref[at : at + size, :].astype(F32)
+
+    @pl.when(pl.program_id(0) == 0)
+    def _():
+        g_out[...] = values(ffn_ref, 0, width)
+        g_down[...] = values(ffn_ref, width, hidden)
+        g_up[...] = values(ffn_ref, width + hidden, hidden).T
+        for i in range(heads // 2):
+            for kind, ref in enumerate((g_query, g_key, g_value)):
+                ref[:, i * pair : (i + 1) * pair] = values(attn_ref, (3 * i + kind) * pair, pair).T
+        tail = values(ffn_ref, width + 2 * hidden, 16)
+        tail_attn = values(attn_ref, 3 * width, 16)
+        rows = (tail[0], tail[1], tail_attn[0], tail_attn[1], tail[2], tail[3])
+        for ref, row in zip(vectors, rows):
+            ref[...] = row
+        for h in range(heads):
+            at = h * up_part
+            g_bup[h : h + 1] = tail[4 + at // lanes : 5 + at // lanes, at % lanes : at % lanes + up_part]
+            for start, ref in ((0, g_bq), (heads * head_part, g_bv)):
+                at = start + h * head_part
+                ref[h : h + 1] = tail_attn[2 + at // lanes : 3 + at // lanes, at % lanes : at % lanes + head_part]
+
+
+def write_results(output, grad_tokens, done_ffn, done_attn, shapes, heads, head_part, up_part):
+    micros, length, features = output.shape
+    steps = 4
+    rows = pl.BlockSpec((micros, length // steps, features), lambda i: (0, i, 0))
+    return pl.pallas_call(
+        functools.partial(results_kernel, heads=heads, head_part=head_part, up_part=up_part),
+        grid=(steps,),
+        in_specs=[rows, rows, once(done_ffn.shape), once(done_attn.shape)],
+        out_specs=[rows, rows] + [full_spec(shape) for shape in shapes],
+        out_shape=[jax.ShapeDtypeStruct(output.shape, BF16)] * 2 + [jax.ShapeDtypeStruct(shape, F32) for shape in shapes],
+        compiler_params=params(),
+        name="results",
+    )(output, grad_tokens, done_ffn, done_attn)
 
 
 def pad_rows(rows, multiple):
@@ -1036,60 +1187,65 @@
     up_part = b_up.shape[1]
     feature_part = b_out.shape[0]
 
-    smalls = [b_query, b_value, b_up, b_out, b_down, gain_attn, shift_attn, gain_ffn, shift_ffn]
-    flat = jnp.concatenate([v.reshape(-1) for v in smalls])
-    small = jnp.pad(flat, (0, -flat.shape[0] % 2048)).reshape(-1, 128)
-    w_all, small_all, x_first = gather_first((w_query, w_key, w_value), small, tokens, ns, nc)
-    small_all = small_all.reshape(2, ns, -1)
-    bias_size, up_size = b_query.size, b_up.size
-    biases = small_all[:, :, : 2 * bias_size].reshape(2, ns, 2, heads, head_part)
-    biases = biases.transpose(2, 0, 3, 1, 4).reshape(2, 2 * heads * head_width).astype(F32)
-    bup = small_all[:, :, 2 * bias_size : 2 * bias_size + up_size].reshape(2, ns, heads, up_part)
-    bup = bup.transpose(0, 2, 1, 3).reshape(2, 1, heads * up_part * ns).astype(F32)
-    at = 2 * bias_size + up_size
-    vectors = small_all[0, :, at : at + 6 * feature_part].reshape(ns, 6, feature_part)
-    vectors = vectors.transpose(1, 0, 2).reshape(6, features).astype(F32)
+    tables = [b_query, b_value, b_up] + [v[None] for v in (b_out, b_down, gain_attn, shift_attn, gain_ffn, shift_ffn)]
+    w_all, small_all, x_first = gather_first((w_query, w_key, w_value), tables, tokens, ns, nc)
+
+    def by_head(row, part):
+        table = small_all[:, :, row : row + heads, :part].transpose(0, 2, 1, 3)
+        return table.reshape(2, heads * part * ns)
+
+    biases = jnp.stack([by_head(0, head_part).reshape(-1), by_head(heads, head_part).reshape(-1)])
+    bup = by_head(2 * heads, up_part)[:, None]
+    vectors = small_all[0, :, 3 * heads : 3 * heads + 6, :feature_part].transpose(1, 0, 2)
+    vectors = vectors.reshape(6, features)
     keys = 2 * nc * half
     aligned = feature_part % 128 == 0
     column_place = place_columns if aligned else place_slot
 
-    def column_shape(w):
-        return (2, w.shape[0], features) if aligned else (2, ns) + w.shape
+    def column_shape(w, rows):
+        return (2, rows, features) if aligned else (2, ns, rows, w.shape[1])
 
     def whole_columns(w):
         if not aligned:
             w = w.transpose(0, 2, 1, 3).reshape(2, w.shape[2], features)
         return w
 
+    ahead = w_down.shape[0] // 4
     plans = [
-        (("ctx", nc, place_distance, True), ("shard", ns, place_rows, False), ("shard", ns, column_place, False)),
-        (("shard", ns, column_place, False),),
+        (("ctx", nc, place_distance, True, 0), ("shard", ns, place_rows, False, 0)),
+        (("shard", ns, column_place, False, ahead),),
     ]
-    sources = [(tokens, w_up, w_out), (w_down,)]
+    sources = [(tokens, w_up), (w_down,)]
     specs = [
-        [once((1, 1, length, features), (1, 0, 0, 0)), once(w_up.shape), once(w_out.shape)],
+        [once((1, 1, length, features), (1, 0, 0, 0)), once(w_up.shape)],
         [once(w_down.shape)],
     ]
     shapes = [
-        ((nc, 2, half, features), (2, features, w_up.shape[1]), column_shape(w_out)),
-        (column_shape(w_down),),
+        ((nc, 2, half, features), (2, features, w_up.shape[1])),
+        (column_shape(w_down, w_down.shape[0] - ahead),),
     ]
+    guests = [(w_out, w_out.shape[0]), (w_down, ahead)]
     x_alls = [x_first.reshape(keys, features), None]
     saved = []
     arrived = []
     for micro in range(micros):
-        normed, k, v, q = front(x_alls[micro], w_all, vectors, biases, head_width, half)
+        guest, guest_rows = guests[micro]
+        normed, k, v, q, early = front(
+            x_alls[micro], w_all, vectors, biases, head_width, half, guest, guest_rows,
+            column_shape(guest, guest_rows), ns, column_place, 6 + micro,
+        )
         mixed, qx, *more = attend_forward(
             q, k, v, head_width, plans[micro], sources[micro], specs[micro], shapes[micro], micro + 1
         )
         if micro == 0:
             x_alls[1] = more.pop(0).reshape(keys, features)
-        arrived += more
+        arrived += [early] + more
         saved.append((normed, k, v, qx, mixed))
-    wu, wo, wd = arrived[0], whole_columns(arrived[1]), whole_columns(arrived[2])
+    wo, wu, down_first, down_rest = arrived
+    wo, down_first, down_rest = whole_columns(wo), whole_columns(down_first), whole_columns(down_rest)
 
     out, grad_middle, grad_mixed, dw, dup, dvec = feed_forward(
-        tokens, [entry[4] for entry in saved], cotangent, wo, wu, wd, bup, vectors, jnp.full((1,), t, jnp.int32)
+        tokens, [entry[4] for entry in saved], cotangent, wo, wu, down_first, down_rest, bup, vectors, jnp.full((1,), t, jnp.int32)
     )
 
     def spread(v, part):
@@ -1104,10 +1260,10 @@
     ).astype(BF16)
 
     width = heads * head_width
-    *starts, dn_first, dw_parts, output = attend_back_rows(
+    *starts, dn_first, other_first, dw_parts, output = attend_back_rows(
         saved[0], grad_mixed, x_alls[0], w_all, head_width, dw, extra, out.reshape(micros, half, features), ns, nc
     )
-    dw_now, db_now, sums, dn_second, dw_done = attend_back_shards(
+    dw_now, db_now, sums, dn_second, other_second, dw_done = attend_back_shards(
         saved[1], grad_mixed, x_alls[1], w_all, head_width, starts, dw_parts, ns, nc
     )
 
@@ -1118,9 +1274,18 @@
         extras.append(pad_rows(jnp.concatenate([sums[:2], as_rows(biases)]), 16 * nc))
     grad_tokens, attn_done = last_sums(
         dw_now.reshape(2, 3 * width, features), jnp.stack(extras).astype(BF16),
-        (dn_first, dn_second), tokens, grad_middle.reshape(micros, half, features), vectors, ns, nc,
-    )
-
+        (dn_first, dn_second, other_first, other_second), tokens, grad_middle.reshape(micros, half, features), vectors, ns, nc,
+    )
+
+    if aligned:
+        weights = (w_query, w_key, w_value, w_out, w_up, w_down, b_query, b_value, b_up)
+        shapes = [v.shape for v in weights] + [(feature_part,)] * 6
+        output, grad_tokens, *grads = write_results(
+            output.reshape(micros, length, features), grad_tokens.reshape(micros, length, features),
+            dw_done.reshape(-1, feature_part), attn_done.reshape(-1, feature_part), shapes, heads, head_part, up_part,
+        )
+        g_query, g_key, g_value, g_out, g_up, g_down, g_bq, g_bv, g_bup, *others = grads
+        return (output[:, None], grad_tokens[:, None], g_query, g_key, g_value, g_out, g_up, g_down, g_bq, g_bv, g_bup, *others)
     output = output.reshape(micros, 1, length, features)
     grad_tokens = grad_tokens.reshape(micros, 1, length, features)
     done_ffn = dw_done.reshape(-1, feature_part).astype(F32)

time: 362 us -> 340 us (0.939)
  local copies, waits for them, and re-layouts: 25.5 us -> 7.32 us
    pallas_call x2 -> x3, Pallas kernels: 21.6 us -> 35.2 us  [the longest x2 29.5 us: front(): pl.pallas_call(functools.partial(front_kernel, q_scale=scale, ns=ns, plac...]
    pallas_call x2, Pallas kernels: 69.4 us -> 61.2 us  [attend_forward(): pl.pallas_call(functools.partial(attend_kernel, kc=kc, width=width, plans...]
    pallas_call x1, Pallas kernels: 34.5 us -> 28 us  [gather_first(): pl.pallas_call(functools.partial(gather_kernel, ns, nc), grid=(1,), in_sp...]
    unnamed x9 -> x0, local copies, waits for them, and re-layouts: 5.71 us -> none
    pallas_call x2, Pallas kernels: 149 us -> 144 us  [attend_back(): pl.pallas_call(functools.partial(attend_back_kernel, width=width, nc=nc,...]
    concatenate x1 -> x0, local copies, waits for them, and re-layouts: 4.08 us -> none  [body(): flat = jnp.concatenate([v.reshape(-1) for v in smalls])]
where the time goes in v1:
time: 340 us; the launch traced here: 339 us
  Pallas kernels  328 us (96%)
  local copies, waits for them, and re-layouts  7.32 us (2%)
    pallas_call x2, Pallas kernels, attend_back(): pl.pallas_call(functools.partial(attend_back_kernel, width=width, nc=nc,...  144 us
    pallas_call x2, Pallas kernels, attend_forward(): pl.pallas_call(functools.partial(attend_kernel, kc=kc, width=width, plans...  61.2 us
    pallas_call x1, Pallas kernels, last_sums(): pl.pallas_call(functools.partial(last_kernel, ns=ns, nc=nc), in_specs=[pl...  34 us
    pallas_call x2, Pallas kernels, front(): pl.pallas_call(functools.partial(front_kernel, q_scale=scale, ns=ns, plac...  29.5 us
    pallas_call x1, Pallas kernels, gather_first(): pl.pallas_call(functools.partial(gather_kernel, ns, nc), grid=(1,), in_sp...  28 us
    pallas_call x1, Pallas kernels, feed_forward(): pl.pallas_call(ffn_kernel, grid_spec=pltpu.PrefetchScalarGridSpec(num_sca...  25.6 us

profile of v1, /device:TPU:0, one launch (start us, length us, event | category | flops | bytes accessed | tf_op | source)
XLA Modules:
  0.0 339.2 jit_solution(2683114549449235846)
XLA Ops:
  0.7 28.0 %gather_first.1 = (bf16[2,3,512,256]{3,2,1,0:T(8,128)(2,1)}, f32[2,4,24,128]{3,2,1,0:T(8,128)}, bf16[4,2,512,512]{3,2,1,0:T(8,128)(2,1)}) custom-call(bf16[128,256]{1,0:T(8,128)(2,1)} %wq_ref.1, bf16[128,256]{1,0:T(8,128)(2,1)} %wk_ref.1, bf16[128,256]{1,0:T(8,128)(2,1)} %wv_ref.1, bf16[2,1,1024,512]{3,2,1,0:T(8,128)(2,1)} %x_ref.3, bf16[4,16]{1,0:T(4,128)(2,1)} %refs_0_.1, ...), custom_call_target="tpu_custom_call" | custom-call | tf_op jit(solution)/shard_map/gather_first/pallas_call | solution.py:266
  28.7 0.8 slice_bitcast_fusion.2
  29.5 0.1 stack_reshape_reshape.6
  29.6 0.1 stack_reshape_reshape.7
  29.7 0.6 pad_maximum_fusion.6.bias_ref
  30.3 1.4 slice_bitcast_fusion.3.vec_ref
  31.7 14.6 %front.2 = (bf16[4096,512]{1,0:T(8,128)(2,1)}, bf16[4096,512]{1,0:T(8,128)(2,1)}, bf16[4096,512]{1,0:T(8,128)(2,1)}, bf16[512,512]{1,0:T(8,128)(2,1)}, bf16[2,256,512]{2,1,0:T(8,128)(2,1)}) custom-call(bf16[4096,512]{1,0:T(8,128)(2,1)} %bitcast.94, bf16[2,3,512,256]{3,2,1,0:T(8,128)(2,1)} %get-tuple-element.76.w_ref.refs_7_, ...), custom_call_target="tpu_custom_call" | custom-call | flops 4294967296 | bytes 16777216 | tf_op jit(solution)/shard_map/front/pallas_call | solution.py:341
  46.3 34.4 %attend_forward.2 = (bf16[512,512]{1,0:T(8,128)(2,1)}, bf16[512,1024]{1,0:T(8,128)(2,1)}, bf16[4,2,512,512]{3,2,1,0:T(8,128)(2,1)}, bf16[2,512,1024]{2,1,0:T(8,128)(2,1)}) custom-call(bf16[512,512]{1,0:T(8,128)(2,1)} %get-tuple-element.78.refs_0_, bf16[4096,512]{1,0:T(8,128)(2,1)} %get-tuple-element.79.refs_1_, bf16[4096,512]{1,0:T(8,128)(2,1)} %get-tuple-element.80.refs_2_, ...), custom_call_target="tpu_custom_call" | custom-call | flops 12884901888 | bytes 8388608 | tf_op jit(solution)/shard_map/attend_forward/pallas_call | solution.py:495
  80.7 14.8 %front.3 = (bf16[4096,512]{1,0:T(8,128)(2,1)}, bf16[4096,512]{1,0:T(8,128)(2,1)}, bf16[4096,512]{1,0:T(8,128)(2,1)}, bf16[512,512]{1,0:T(8,128)(2,1)}, bf16[2,256,512]{2,1,0:T(8,128)(2,1)}) custom-call(bf16[4096,512]{1,0:T(8,128)(2,1)} %bitcast.98, bf16[2,3,512,256]{3,2,1,0:T(8,128)(2,1)} %get-tuple-element.76.w_ref.refs_7_, ...), custom_call_target="tpu_custom_call" | custom-call | flops 4294967296 | bytes 16777216 | tf_op jit(solution)/shard_map/front/pallas_call | solution.py:341
  95.6 26.8 %attend_forward.3 = (bf16[512,512]{1,0:T(8,128)(2,1)}, bf16[512,1024]{1,0:T(8,128)(2,1)}, bf16[2,768,512]{2,1,0:T(8,128)(2,1)}) custom-call(bf16[512,512]{1,0:T(8,128)(2,1)} %get-tuple-element.84.refs_0_, bf16[4096,512]{1,0:T(8,128)(2,1)} %get-tuple-element.85.refs_1_, bf16[4096,512]{1,0:T(8,128)(2,1)} %get-tuple-element.86.refs_2_, bf16[1024,128]{1,0:T(8,128)(2,1)} %refs_3_.3), custom_call_target="tpu_custom_call" | custom-call | flops 12884901888 | bytes 8388608 | tf_op jit(solution)/shard_map/attend_forward/pallas_call | solution.py:495
  122.4 0.8 slice_bitcast_fusion
  123.2 0.7 broadcast_in_dim_reshape.3.bup_ref
  123.8 25.6 %feed_forward.1 = (bf16[1024,512]{1,0:T(8,128)(2,1)}, f32[1024,512]{1,0:T(8,128)}, bf16[1024,512]{1,0:T(8,128)(2,1)}, bf16[2,2304,512]{2,1,0:T(8,128)(2,1)}, f32[2,1,1024]{2,1,0:T(1,128)}, /*index=5*/f32[8,512]{1,0:T(8,128)}) custom-call(s32[1]{0:T(128)} %bitcast.12.where_ref, bf16[2,1,1024,512]{3,2,1,0:T(8,128)(2,1)} %x_ref.3, ...), custom_call_target="tpu_custom_call" | custom-call | flops 14495514624 | bytes 23592960 | tf_op jit(solution)/shard_map/feed_forward/pallas_call | solution.py:1015
  149.5 0.7 convert.67
  150.3 0.1 reshape_reshape.8
  150.5 0.1 reshape_reshape.9
  150.6 0.7 slice.79
  151.5 0.7 pad_maximum_fusion.refs_10_
  152.1 74.1 %attend_back.2 = (f32[4,3,128,512]{3,2,1,0:T(8,128)}, f32[4,8,128]{2,1,0:T(8,128)}, f32[8,512]{1,0:T(8,128)}, f32[512,512]{1,0:T(8,128)}, bf16[512,512]{1,0:T(8,...) custom-call(bf16[512,1024]{1,0:T(8,128)(2,1)} %get-tuple-element.81.refs_0_, ...), custom_call_target="tpu_custom_call" | custom-call | flops 32212254720 | bytes 16777216 | tf_op jit(solution)/shard_map/attend_back/pallas_call | solution.py:868
  226.2 69.9 %attend_back.3 = (bf16[4,3,128,512]{3,2,1,0:T(8,128)(2,1)}, f32[4,8,128]{2,1,0:T(8,128)}, f32[8,512]{1,0:T(8,128)}, f32[512,512]{1,0:T(8,128)}, bf16[512,512]{1,0:T(8,128)(2,1)}, /*index=5*/bf16[4,592,128]{2,1,0:T(8,128)(2,1)}) custom-call(bf16[512,1024]{1,0:T(8,128)(2,1)} %get-tuple-element.99.refs_0_, bf16[4096,512]{1,0:T(8,128)(2,1)} %get-tuple-element.85.refs_1_, ...), custom_call_target="tpu_custom_call" | custom-call | flops 32212254720 | bytes 16777216 | tf_op jit(solution)/shard_map/attend_back/pallas_call | solution.py:868
  296.1 0.7 slice.80
  296.9 0.1 reshape_squeeze.26
  296.9 0.1 reshape.104
  297.0 0.1 reshape_squeeze.27
  297.1 0.1 reshape.105
  297.4 0.1 reshape.106
  297.5 0.1 reshape_squeeze.29
  297.6 0.1 reshape.107
  297.8 0.7 slice.81
  298.7 0.7 pad_maximum_fusion.1.extra_ref
  299.3 34.0 %last_sums.1 = (bf16[2,2,512,512]{3,2,1,0:T(8,128)(2,1)}, bf16[4,208,128]{2,1,0:T(8,128)(2,1)}) custom-call(bf16[2,768,512]{2,1,0:T(8,128)(2,1)} %bitcast.76, bf16[2,64,512]{2,1,0:T(8,128)(2,1)} %pad_maximum_fusion.1.extra_ref, f32[512,512]{1,0:T(8,128)} %get-tuple-element.108.dn0_ref, f32[512,512]{1,0:T(8,128)} %get-tuple-element.109.dn1_ref, ...), custom_call_target="tpu_custom_call" | custom-call | tf_op jit(solution)/shard_map/last_sums/pallas_call | solution.py:1106
  333.3 5.7 %results.1 = (bf16[2,1024,512]{2,1,0:T(8,128)(2,1)}, bf16[2,1024,512]{2,1,0:T(8,128)(2,1)}, f32[128,256]{1,0:T(8,128)}, f32[128,256]{1,0:T(8,128)}, f32[128,256]...) custom-call(bf16[2,1024,512]{2,1,0:T(8,128)(2,1)} %bitcast.74, ...), custom_call_target="tpu_custom_call" | custom-call | tf_op jit(solution)/shard_map/results/pallas_call | solution.py:1161
  (23 shorter events, 0.9 us)

commit v2 on v1

--- a/solution.py
+++ b/solution.py
@@ -125,9 +125,25 @@
             self.first(d).wait_recv()
             self.cross(d).start()
 
-    def finish(self):
-        for d in range(1, self.count):
+    def relay(self, h):
+        size = self.target.shape[2] // 2
+        rows = pl.ds(h * size, size)
+        i = (3, 0)[h]
+        where = {self.name: self.me ^ (2 - h)}
+        return send(
+            self.target.at[1 + h, 0, rows, :], self.target.at[3, 0, rows, :], self.out_sem.at[i], self.in_sem.at[i], where
+        )
+
+    def forward_relayed(self):
+        for h in range(2):
+            self.relay(h).wait_recv()
+        self.cross(3).start()
+
+    def finish(self, relayed=False):
+        for d in range(1, 3 if relayed else self.count):
             self.first(d).wait_send()
+        for h in range(2 if relayed else 0):
+            self.relay(h).wait_send()
         for d in self.crossed():
             self.cross(d).wait()
         for copy in self.locals():
@@ -157,11 +173,11 @@
     return [dma((count,)), dma((count,)), dma((count,)), dma((count,)), dma((2,))]
 
 
-def gather_kernel(ns, nc, wq_ref, wk_ref, wv_ref, x_block, *refs):
-    tables, (w_out, small_out, x_out, small_ref), sems = refs[:-17], refs[-17:-13], refs[-13:]
+def gather_kernel(ns, nc, place, wq_ref, wk_ref, wv_ref, wo_ref, x_block, *refs):
+    tables, (w_out, wo_out, small_out, x_out, small_ref), sems = refs[:-18], refs[-18:-13], refs[-13:]
     w_send, w_recv, s_send, s_recv, x_send, x_recv, wt_send, wt_recv, st_send, st_recv, xt_send, xt_recv, local = sems
-    w_refs = (wq_ref, wk_ref, wv_ref)
-    kinds = range(3)
+    w_refs = (wq_ref, wk_ref, wv_ref, wo_ref)
+    kinds = range(4)
     x_ref = x_block.at[0, 0]
     s = lax.axis_index("shard")
     c = lax.axis_index("ctx")
@@ -181,6 +197,8 @@
     greet_wait(peers)
 
     def w_rows(part, kind, owner):
+        if kind == 3:
+            return place(wo_out, part, owner, 0)
         return w_out.at[part, kind, pl.ds(pl.multiple_of(owner * depth, depth), depth), :]
 
     def x_rows(which):
@@ -217,9 +235,9 @@
     last.append(begin(small_ref, small_out.at[1, s], st_send.at[0], st_recv.at[0], {"tp": other}))
     locals_ = [pltpu.make_async_copy(w_refs[k], w_rows(0, k, s), local.at[k]) for k in kinds]
     locals_ += [
-        pltpu.make_async_copy(small_ref, small_out.at[0, s], local.at[3]),
-        pltpu.make_async_copy(x_rows(t), x_out.at[0, 0], local.at[4]),
-        pltpu.make_async_copy(x_rows(other), x_out.at[0, 1], local.at[5]),
+        pltpu.make_async_copy(small_ref, small_out.at[0, s], local.at[4]),
+        pltpu.make_async_copy(x_rows(t), x_out.at[0, 0], local.at[5]),
+        pltpu.make_async_copy(x_rows(other), x_out.at[0, 1], local.at[6]),
     ]
     for copy in locals_:
         copy.start()
@@ -256,7 +274,7 @@
         copy.wait()
 
 
-def gather_first(weights, tables, tokens, ns, nc):
+def gather_first(weights, tables, tokens, place, shape, ns, nc):
     depth, width = weights[0].shape
     length, features = tokens.shape[2:]
     rows = -(-sum(table.shape[0] for table in tables) // 8) * 8
@@ -264,18 +282,19 @@
     dma = pltpu.SemaphoreType.DMA
     vmem = pl.BlockSpec(memory_space=pltpu.VMEM)
     return pl.pallas_call(
-        functools.partial(gather_kernel, ns, nc),
+        functools.partial(gather_kernel, ns, nc, place),
         grid=(1,),
-        in_specs=[vmem] * 3 + [once((1, 1, length, features))] + [vmem] * len(tables),
-        out_specs=[pl.BlockSpec(memory_space=pl.ANY)] * 3,
+        in_specs=[vmem] * 4 + [once((1, 1, length, features))] + [vmem] * len(tables),
+        out_specs=[pl.BlockSpec(memory_space=pl.ANY)] * 4,
         out_shape=[
             jax.ShapeDtypeStruct((2, 3, ns * depth, width), BF16),
+            jax.ShapeDtypeStruct(shape, BF16),
             jax.ShapeDtypeStruct((2, ns, rows, lanes), F32),
             jax.ShapeDtypeStruct((nc, 2, length // 2, features), BF16),
         ],
         scratch_shapes=[pltpu.VMEM((rows, lanes), F32)]
-        + [dma((3, ns)), dma((3, ns)), dma((ns,)), dma((ns,)), dma((nc, 2)), dma((nc, 2))]
-        + [dma((3, ns)), dma((3, ns)), dma((ns,)), dma((ns,)), dma((nc,)), dma((nc,)), dma((6,))],
+        + [dma((4, ns)), dma((4, ns)), dma((ns,)), dma((ns,)), dma((nc, 2)), dma((nc, 2))]
+        + [dma((4, ns)), dma((4, ns)), dma((ns,)), dma((ns,)), dma((nc,)), dma((nc,)), dma((7,))],
         compiler_params=params(collective_id=0, has_side_effects=True),
         name="gather_first",
     )(*weights, tokens, *tables)
@@ -308,7 +327,8 @@
     x_ref, w_ref, vec_ref, bias_ref, guest_ref, n_ref, k_ref, v_ref, q_ref, guest_all, *sems, q_scale, ns, place, size
 ):
     step = pl.program_id(0)
-    gather = Gather("shard", ns, guest_ref.at[pl.ds(0, size), :], None, guest_all, place, sems)
+    part = guest_ref.at[:, pl.ds(0, size)] if place is place_rows else guest_ref.at[pl.ds(0, size), :]
+    gather = Gather("shard", ns, part, None, guest_all, place, sems)
 
     peers = [("tp", 2), ("shard", ns)]
 
@@ -406,6 +426,8 @@
                 half = source.shape[0] // 2
                 theirs = source.at[pl.ds(pl.multiple_of((1 - t) * half, half), half), :]
                 source = source.at[pl.ds(pl.multiple_of(t * half, half), half), :]
+            elif start and place is place_rows:
+                source = source.at[:, pl.ds(start, source.shape[1] - start)]
             elif start:
                 source = source.at[pl.ds(start, source.shape[0] - start), :]
             found.append(Gather(name, number, source, theirs, targets[i], place, sems[5 * i : 5 * i + 5]))
@@ -415,6 +437,7 @@
 
     peers = [("tp", 2)] + list(counts.items())
     far = counts.get("ctx", 1) - 1
+    relayed = far == 3
 
     @pl.when(step == 0)
     def _():
@@ -449,8 +472,11 @@
     @pl.when(step == 2)
     def _():
         for gather in gathers("ctx"):
-            gather.first(far).start()
+            if not relayed:
+                gather.first(far).start()
             gather.forward(range(1, far))
+            for h in range(2 if relayed else 0):
+                gather.relay(h).start()
 
     @pl.when(step == last)
     def _():
@@ -480,10 +506,13 @@
             for gather in gathers("shard"):
                 gather.forward()
             for gather in gathers("ctx"):
-                gather.forward([far])
+                if relayed:
+                    gather.forward_relayed()
+                else:
+                    gather.forward([far])
         for name in counts:
             for gather in gathers(name):
-                gather.finish()
+                gather.finish(relayed and name == "ctx")
 
 
 def attend_forward(q, k, v, width, plans, sources, source_specs, shapes, number):
@@ -945,17 +974,20 @@
 
 
 def ffn_kernel(
-    where_ref, x_ref, o0_ref, o1_ref, g_ref, w_out, w_up, down_first, down_rest, bup_ref, vec_ref,
-    out_ref, gm_ref, gx_ref, dw_ref, dup_ref, dvec_ref, dw_acc, w_down,
+    where_ref, x_ref, o0_ref, o1_ref, g_ref, w_out, up_first, up_rest, down_first, down_rest, bup_ref, vec_ref,
+    out_ref, gm_ref, gx_ref, dw_ref, extra_ref, dw_acc, w_up, w_down, dup_ref, dvec_ref, extra, *, ns, up_part,
 ):
     step = pl.program_id(0)
     steps = pl.num_programs(0)
     b_out, b_down, gain, shift = (vec_ref[i : i + 1, :] for i in (0, 1, 4, 5))
     hw = w_out.shape[1]
-    hidden = w_up.shape[2]
+    hidden = bup_ref.shape[2]
 
     @pl.when(step == 0)
     def _():
+        split = up_first.shape[2]
+        w_up[:, :, :split] = up_first[...]
+        w_up[:, :, split:] = up_rest[...]
         split = down_first.shape[1]
         w_down[:, :split] = down_first[...]
         w_down[:, split:] = down_rest[...]
@@ -1000,20 +1032,39 @@
     @pl.when(step == steps - 1)
     def _():
         dw_ref[...] = dw_acc[...].astype(BF16)
-
-
-def feed_forward(tokens, mixed, cotangent, w_out, w_up, down_first, down_rest, b_up, vectors, where):
+        features = dvec_ref.shape[1]
+        extra[...] = jnp.zeros_like(extra)
+        for part in range(2):
+            extra[part, 0:4] = dvec_ref[0:4]
+            for r in range(hidden // features):
+                extra[part, 4 + r : 5 + r] = spread_columns(dup_ref[part], r, up_part, ns, features)
+        extra_ref[...] = extra[...].astype(BF16)
+
+
+def spread_columns(row, r, size, ns, features):
+    count = row.shape[1]
+    width = features // ns
+    column = lax.broadcasted_iota(jnp.int32, (1, features), 1)
+    shard = column // width
+    place = r * width + column % width
+    source = (place // size) * (size * ns) + shard * size + place % size
+    chosen = jnp.where(lax.broadcasted_iota(jnp.int32, (count, features), 0) == source, 1.0, 0.0).astype(BF16)
+    return dot_nn(jnp.broadcast_to(row.astype(BF16), (16, count)), chosen)[0:1]
+
+
+def feed_forward(tokens, mixed, cotangent, w_out, up_first, up_rest, down_first, down_rest, b_up, vectors, where, up_part, ns, nc):
     micros, _, length, features = tokens.shape
     block = 256
     half = length // 2
     each = half // block
     rows = micros * half
-    hw, hidden = w_out.shape[1], w_up.shape[2]
+    hw, hidden = w_out.shape[1], b_up.shape[2]
     total = hw + 2 * hidden
+    more = (2, 16 * nc, features)
     row_spec = pl.BlockSpec((block, features), lambda i, t: (i, 0))
     input_spec = pl.BlockSpec((1, 1, block, features), lambda i, t: (i // each, 0, t[0] * each + i % each, 0))
     return pl.pallas_call(
-        ffn_kernel,
+        functools.partial(ffn_kernel, ns=ns, up_part=up_part),
         grid_spec=pltpu.PrefetchScalarGridSpec(
             num_scalar_prefetch=1,
             grid=(rows // block,),
@@ -1023,33 +1074,36 @@
                 pl.BlockSpec((block, 2 * hw), lambda i, t: (jnp.maximum(i - each, 0), 0)),
                 input_spec,
             ]
-            + [once(w.shape) for w in (w_out, w_up, down_first, down_rest)]
+            + [once(w.shape) for w in (w_out, up_first, up_rest, down_first, down_rest)]
             + [once(b_up.shape), once(vectors.shape)],
             out_specs=[row_spec] * 3
-            + [full_spec((2, total, features)), full_spec((2, 1, hidden)), full_spec((8, features))],
-            scratch_shapes=[pltpu.VMEM((2, total, features), F32), pltpu.VMEM((2, hidden, features), BF16)],
+            + [once((2, total, features)), full_spec(more)],
+            scratch_shapes=[
+                pltpu.VMEM((2, total, features), F32), pltpu.VMEM((2, features, hidden), BF16),
+                pltpu.VMEM((2, hidden, features), BF16), pltpu.VMEM((2, 1, hidden), F32), pltpu.VMEM((8, features), F32),
+                pltpu.VMEM(more, F32),
+            ],
         ),
         out_shape=[
             jax.ShapeDtypeStruct((rows, features), BF16),
             jax.ShapeDtypeStruct((rows, features), F32),
             jax.ShapeDtypeStruct((rows, 2 * hw), BF16),
             jax.ShapeDtypeStruct((2, total, features), BF16),
-            jax.ShapeDtypeStruct((2, 1, hidden), F32),
-            jax.ShapeDtypeStruct((8, features), F32),
+            jax.ShapeDtypeStruct(more, BF16),
         ],
         compiler_params=params(),
         cost_estimate=pl.CostEstimate(
             flops=12 * rows * total * features, bytes_accessed=20 * total * features, transcendentals=4 * rows * hidden
         ),
         name="feed_forward",
-    )(where, tokens, *mixed, cotangent, w_out, w_up, down_first, down_rest, b_up, vectors)
+    )(where, tokens, *mixed, cotangent, w_out, up_first, up_rest, down_first, down_rest, b_up, vectors)
 
 
 def last_kernel(
-    dw_ref, extra_ref, dn0_ref, dn1_ref, other0_ref, other1_ref, x_ref, gm_ref, vec_ref,
+    dw_ref, db_ref, sums_ref, dn0_ref, dn1_ref, other0_ref, other1_ref, x_ref, gm_ref, vec_ref,
     grad_ref, blocks_ref,
-    dn_received, w_received, w_total, w_blocks, z_parts, z_received,
-    dn_out, dn_in, wtp_out, wtp_in, wctx_out, wctx_in, z_out, z_in, back_out, back_in, row_out, row_in, *, ns, nc,
+    extra, extra_ref, dn_received, w_received, w_total, w_blocks, z_parts, z_received,
+    dn_out, dn_in, wtp_out, wtp_in, wctx_out, wctx_in, z_out, z_in, back_out, back_in, row_out, row_in, *, ns, nc, head_part,
 ):
     t = lax.axis_index("tp")
     half = grad_ref.shape[2]
@@ -1083,7 +1137,17 @@
         lax.fori_loop(0, half // size, one, 0)
         row(micro).start()
 
-    greet([("tp", 2), ("ctx", nc), ("shard", ns)])
+    peers = [("tp", 2), ("ctx", nc), ("shard", ns)]
+    greet_first(peers)
+    features = sums_ref.shape[1]
+    each = db_ref.shape[0] // 2
+    extra[...] = jnp.zeros_like(extra)
+    for part in range(2):
+        extra[part, 0:2] = sums_ref[0:2]
+        biases = [db_ref[part * each + i, kind : kind + 1] for kind in range(2) for i in range(each)]
+        extra[part, 2:3] = spread_columns(jnp.concatenate(biases, axis=1), 0, head_part, ns, features)
+    extra_ref[...] = extra[...].astype(BF16)
+    greet_wait(peers)
     rows.start()
     for copy in others:
         copy.start()
@@ -1098,28 +1162,29 @@
         row(micro).wait()
 
 
-def last_sums(dw, extra, dn, x, grad_middle, vectors, ns, nc):
+def last_sums(dw, db, sums, dn, x, grad_middle, vectors, head_part, ns, nc):
     main, features = dw.shape[1:]
-    rows = main + extra.shape[1]
+    more = (2, 16 * nc, features)
+    rows = main + more[1]
     micros, half, _ = grad_middle.shape
     size, part = rows // nc, features // ns
     return pl.pallas_call(
-        functools.partial(last_kernel, ns=ns, nc=nc),
-        in_specs=[pl.BlockSpec(memory_space=pltpu.VMEM)] * 9,
+        functools.partial(last_kernel, ns=ns, nc=nc, head_part=head_part),
+        in_specs=[pl.BlockSpec(memory_space=pltpu.VMEM)] * 10,
         out_specs=[pl.BlockSpec(memory_space=pltpu.VMEM)] * 2,
         out_shape=[
             jax.ShapeDtypeStruct((micros, 2, half, features), BF16),
             jax.ShapeDtypeStruct((nc, size, part), BF16),
         ],
         scratch_shapes=[
-            pltpu.VMEM((micros, half, features), BF16),
+            pltpu.VMEM(more, F32), pltpu.VMEM(more, BF16), pltpu.VMEM((micros, half, features), BF16),
             pltpu.VMEM((rows, features), BF16), pltpu.VMEM((rows, features), BF16), pltpu.VMEM((nc, size, features), BF16),
             pltpu.VMEM((ns, size, part), BF16), pltpu.VMEM((ns, size, part), BF16),
             *axis_sems(micros, 2, nc, ns, nc, micros),
         ],
         compiler_params=params(collective_id=5, has_side_effects=True),
         name="last_sums",
-    )(dw, extra, *dn, x, grad_middle, vectors)
+    )(dw, db, sums, *dn, x, grad_middle, vectors)
 
 
 def results_kernel(out_ref, grad_ref, ffn_ref, attn_ref, *refs, heads, head_part, up_part):
@@ -1188,7 +1253,21 @@
     feature_part = b_out.shape[0]
 
     tables = [b_query, b_value, b_up] + [v[None] for v in (b_out, b_down, gain_attn, shift_attn, gain_ffn, shift_ffn)]
-    w_all, small_all, x_first = gather_first((w_query, w_key, w_value), tables, tokens, ns, nc)
+    keys = 2 * nc * half
+    aligned = feature_part % 128 == 0
+    column_place = place_columns if aligned else place_slot
+
+    def column_shape(w, rows):
+        return (2, rows, features) if aligned else (2, ns, rows, w.shape[1])
+
+    def whole_columns(w):
+        if not aligned:
+            w = w.transpose(0, 2, 1, 3).reshape(2, w.shape[2], features)
+        return w
+
+    w_all, wo, small_all, x_first = gather_first(
+        (w_query, w_key, w_value, w_out), tables, tokens, column_place, column_shape(w_out, w_out.shape[0]), ns, nc
+    )
 
     def by_head(row, part):
         table = small_all[:, :, row : row + heads, :part].transpose(0, 2, 1, 3)
@@ -1198,21 +1277,9 @@
     bup = by_head(2 * heads, up_part)[:, None]
     vectors = small_all[0, :, 3 * heads : 3 * heads + 6, :feature_part].transpose(1, 0, 2)
     vectors = vectors.reshape(6, features)
-    keys = 2 * nc * half
-    aligned = feature_part % 128 == 0
-    column_place = place_columns if aligned else place_slot
-
-    def column_shape(w, rows):
-        return (2, rows, features) if aligned else (2, ns, rows, w.shape[1])
-
-    def whole_columns(w):
-        if not aligned:
-            w = w.transpose(0, 2, 1, 3).reshape(2, w.shape[2], features)
-        return w
-
-    ahead = w_down.shape[0] // 4
+    ahead, up_ahead = w_down.shape[0] // 4, w_up.shape[1] // 4
     plans = [
-        (("ctx", nc, place_distance, True, 0), ("shard", ns, place_rows, False, 0)),
+        (("ctx", nc, place_distance, True, 0), ("shard", ns, place_rows, False, up_ahead)),
         (("shard", ns, column_place, False, ahead),),
     ]
     sources = [(tokens, w_up), (w_down,)]
@@ -1221,18 +1288,21 @@
         [once(w_down.shape)],
     ]
     shapes = [
-        ((nc, 2, half, features), (2, features, w_up.shape[1])),
+        ((nc, 2, half, features), (2, features, w_up.shape[1] - up_ahead)),
         (column_shape(w_down, w_down.shape[0] - ahead),),
     ]
-    guests = [(w_out, w_out.shape[0]), (w_down, ahead)]
+    guests = [
+        (w_up, up_ahead, (2, features, up_ahead), place_rows),
+        (w_down, ahead, column_shape(w_down, ahead), column_place),
+    ]
     x_alls = [x_first.reshape(keys, features), None]
     saved = []
     arrived = []
     for micro in range(micros):
-        guest, guest_rows = guests[micro]
+        guest, guest_rows, guest_shape, guest_place = guests[micro]
         normed, k, v, q, early = front(
             x_alls[micro], w_all, vectors, biases, head_width, half, guest, guest_rows,
-            column_shape(guest, guest_rows), ns, column_place, 6 + micro,
+            guest_shape, ns, guest_place, 6 + micro,
         )
         mixed, qx, *more = attend_forward(
             q, k, v, head_width, plans[micro], sources[micro], specs[micro], shapes[micro], micro + 1
@@ -1241,23 +1311,13 @@
             x_alls[1] = more.pop(0).reshape(keys, features)
         arrived += [early] + more
         saved.append((normed, k, v, qx, mixed))
-    wo, wu, down_first, down_rest = arrived
+    up_first, up_rest, down_first, down_rest = arrived
     wo, down_first, down_rest = whole_columns(wo), whole_columns(down_first), whole_columns(down_rest)
 
-    out, grad_middle, grad_mixed, dw, dup, dvec = feed_forward(
-        tokens, [entry[4] for entry in saved], cotangent, wo, wu, down_first, down_rest, bup, vectors, jnp.full((1,), t, jnp.int32)
-    )
-
-    def spread(v, part):
-        return v.reshape(heads, ns, part).transpose(1, 0, 2).reshape(ns, -1)
-
-    def as_rows(v):
-        count = v.shape[1] // feature_part
-        return v.reshape(ns, count, feature_part).transpose(1, 0, 2).reshape(count, features)
-
-    extra = jnp.stack(
-        [pad_rows(jnp.concatenate([dvec[:4], as_rows(spread(dup[part, 0], up_part))]), 16 * nc) for part in range(2)]
-    ).astype(BF16)
+    out, grad_middle, grad_mixed, dw, extra = feed_forward(
+        tokens, [entry[4] for entry in saved], cotangent, wo, up_first, up_rest, down_first, down_rest, bup, vectors,
+        jnp.full((1,), t, jnp.int32), up_part, ns, nc,
+    )
 
     width = heads * head_width
     *starts, dn_first, other_first, dw_parts, output = attend_back_rows(
@@ -1267,14 +1327,9 @@
         saved[1], grad_mixed, x_alls[1], w_all, head_width, starts, dw_parts, ns, nc
     )
 
-    db_now = db_now[:, :2].reshape(2, -1, 2, 2 * head_width).transpose(0, 2, 1, 3).reshape(2, 2, width)
-    extras = []
-    for part in range(2):
-        biases = jnp.concatenate([spread(db_now[part, 0], head_part), spread(db_now[part, 1], head_part)], axis=1)
-        extras.append(pad_rows(jnp.concatenate([sums[:2], as_rows(biases)]), 16 * nc))
     grad_tokens, attn_done = last_sums(
-        dw_now.reshape(2, 3 * width, features), jnp.stack(extras).astype(BF16),
-        (dn_first, dn_second, other_first, other_second), tokens, grad_middle.reshape(micros, half, features), vectors, ns, nc,
+        dw_now.reshape(2, 3 * width, features), db_now, sums,
+        (dn_first, dn_second, other_first, other_second), tokens, grad_middle.reshape(micros, half, features), vectors, head_part, ns, nc,
     )
 
     if aligned:

time: 340 us -> 340 us (level)
  Pallas kernels: 328 us -> 334 us
  local copies, waits for them, and re-layouts: 7.32 us -> 3.85 us
    pallas_call x3, Pallas kernels: 87.6 us -> 92.8 us  [the longest x1 34.4 us: last_sums(): pl.pallas_call(functools.partial(last_kernel, ns=ns, nc=nc, head_part=hea...]
where the time goes in v2:
time: 340 us; the launch traced here: 339 us
  Pallas kernels  334 us (98%)
  local copies, waits for them, and re-layouts  3.85 us (1%)
    pallas_call x2, Pallas kernels, attend_back(): pl.pallas_call(functools.partial(attend_back_kernel, width=width, nc=nc,...  144 us
    pallas_call x2, Pallas kernels, attend_forward(): pl.pallas_call(functools.partial(attend_kernel, kc=kc, width=width, plans...  58.7 us
    pallas_call x1, Pallas kernels, last_sums(): pl.pallas_call(functools.partial(last_kernel, ns=ns, nc=nc, head_part=hea...  34.4 us
    pallas_call x2, Pallas kernels, front(): pl.pallas_call(functools.partial(front_kernel, q_scale=scale, ns=ns, plac...  32.2 us
    pallas_call x1, Pallas kernels, gather_first(): pl.pallas_call(functools.partial(gather_kernel, ns, nc, place), grid=(1,)...  31.3 us
    pallas_call x1, Pallas kernels, feed_forward(): pl.pallas_call(functools.partial(ffn_kernel, ns=ns, up_part=up_part), gri...  27.1 us

profile of v2, /device:TPU:0, one launch (start us, length us, event | category | flops | bytes accessed | tf_op | source)
XLA Modules:
  0.0 339.0 jit_solution(2733769411655371402)
XLA Ops:
  0.7 31.3 %gather_first.1 = (bf16[2,3,512,256]{3,2,1,0:T(8,128)(2,1)}, bf16[2,256,512]{2,1,0:T(8,128)(2,1)}, f32[2,4,24,128]{3,2,1,0:T(8,128)}, bf16[4,2,512,512]{3,2,1,0:T(8,128)(2,1)}) custom-call(bf16[128,256]{1,0:T(8,128)(2,1)} %wq_ref.1, bf16[128,256]{1,0:T(8,128)(2,1)} %wk_ref.1, bf16[128,256]{1,0:T(8,128)(2,1)} %wv_ref.1, bf16[256,128]{1,0:T(8,128)(2,1)} %wo_ref.1, ...), custom_call_target="tpu_custom_call" | custom-call | tf_op jit(solution)/shard_map/gather_first/pallas_call | solution.py:284
  31.9 1.4 slice_bitcast_fusion.3.vec_ref
  33.3 0.8 slice_bitcast_fusion
  34.1 0.8 slice_bitcast_fusion.2
  34.9 0.1 stack_reshape_reshape.6
  35.0 0.7 broadcast_in_dim_reshape.3.bup_ref
  35.7 0.1 stack_reshape_reshape.7
  35.8 0.6 pad_maximum_fusion.bias_ref
  36.4 17.3 %front.2 = (bf16[4096,512]{1,0:T(8,128)(2,1)}, bf16[4096,512]{1,0:T(8,128)(2,1)}, bf16[4096,512]{1,0:T(8,128)(2,1)}, bf16[512,512]{1,0:T(8,128)(2,1)}, bf16[2,512,256]{2,1,0:T(8,128)(2,1)}) custom-call(bf16[4096,512]{1,0:T(8,128)(2,1)} %bitcast.46, bf16[2,3,512,256]{3,2,1,0:T(8,128)(2,1)} %get-tuple-element.76.w_ref.refs_7_, ...), custom_call_target="tpu_custom_call" | custom-call | flops 4294967296 | bytes 16777216 | tf_op jit(solution)/shard_map/front/pallas_call | solution.py:361
  53.7 31.9 %attend_forward.2 = (bf16[512,512]{1,0:T(8,128)(2,1)}, bf16[512,1024]{1,0:T(8,128)(2,1)}, bf16[4,2,512,512]{3,2,1,0:T(8,128)(2,1)}, bf16[2,512,768]{2,1,0:T(8,128)(2,1)}) custom-call(bf16[512,512]{1,0:T(8,128)(2,1)} %get-tuple-element.78.refs_0_, bf16[4096,512]{1,0:T(8,128)(2,1)} %get-tuple-element.79.refs_1_, bf16[4096,512]{1,0:T(8,128)(2,1)} %get-tuple-element.80.refs_2_, ...), custom_call_target="tpu_custom_call" | custom-call | flops 12884901888 | bytes 8388608 | tf_op jit(solution)/shard_map/attend_forward/pallas_call | solution.py:524
  85.6 14.9 %front.3 = (bf16[4096,512]{1,0:T(8,128)(2,1)}, bf16[4096,512]{1,0:T(8,128)(2,1)}, bf16[4096,512]{1,0:T(8,128)(2,1)}, bf16[512,512]{1,0:T(8,128)(2,1)}, bf16[2,256,512]{2,1,0:T(8,128)(2,1)}) custom-call(bf16[4096,512]{1,0:T(8,128)(2,1)} %bitcast.50, bf16[2,3,512,256]{3,2,1,0:T(8,128)(2,1)} %get-tuple-element.76.w_ref.refs_7_, ...), custom_call_target="tpu_custom_call" | custom-call | flops 4294967296 | bytes 16777216 | tf_op jit(solution)/shard_map/front/pallas_call | solution.py:361
  100.5 26.8 %attend_forward.3 = (bf16[512,512]{1,0:T(8,128)(2,1)}, bf16[512,1024]{1,0:T(8,128)(2,1)}, bf16[2,768,512]{2,1,0:T(8,128)(2,1)}) custom-call(bf16[512,512]{1,0:T(8,128)(2,1)} %get-tuple-element.84.refs_0_, bf16[4096,512]{1,0:T(8,128)(2,1)} %get-tuple-element.85.refs_1_, bf16[4096,512]{1,0:T(8,128)(2,1)} %get-tuple-element.86.refs_2_, bf16[1024,128]{1,0:T(8,128)(2,1)} %refs_3_.3), custom_call_target="tpu_custom_call" | custom-call | flops 12884901888 | bytes 8388608 | tf_op jit(solution)/shard_map/attend_forward/pallas_call | solution.py:524
  127.3 27.1 %feed_forward.1 = (bf16[1024,512]{1,0:T(8,128)(2,1)}, f32[1024,512]{1,0:T(8,128)}, bf16[1024,512]{1,0:T(8,128)(2,1)}, bf16[2,2304,512]{2,1,0:T(8,128)(2,1)}, bf16[2,64,512]{2,1,0:T(8,128)(2,1)}) custom-call(s32[1]{0:T(128)} %bitcast.12.where_ref, bf16[2,1,1024,512]{3,2,1,0:T(8,128)(2,1)} %x_ref.3, bf16[512,512]{1,0:T(8,128)(2,1)} %get-tuple-element.82.o0_ref.refs_4_, ...), custom_call_target="tpu_custom_call" | custom-call | flops 14495514624 | bytes 23592960 | tf_op jit(solution)/shard_map/feed_forward/pallas_call | solution.py:1066
  154.4 74.3 %attend_back.2 = (f32[4,3,128,512]{3,2,1,0:T(8,128)}, f32[4,8,128]{2,1,0:T(8,128)}, f32[8,512]{1,0:T(8,128)}, f32[512,512]{1,0:T(8,128)}, bf16[512,512]{1,0:T(8,...) custom-call(bf16[512,1024]{1,0:T(8,128)(2,1)} %get-tuple-element.81.refs_0_, ...), custom_call_target="tpu_custom_call" | custom-call | flops 32212254720 | bytes 16777216 | tf_op jit(solution)/shard_map/attend_back/pallas_call | solution.py:897
  228.7 69.9 %attend_back.3 = (bf16[4,3,128,512]{3,2,1,0:T(8,128)(2,1)}, f32[4,8,128]{2,1,0:T(8,128)}, f32[8,512]{1,0:T(8,128)}, f32[512,512]{1,0:T(8,128)}, bf16[512,512]{1,0:T(8,128)(2,1)}, /*index=5*/bf16[4,592,128]{2,1,0:T(8,128)(2,1)}) custom-call(bf16[512,1024]{1,0:T(8,128)(2,1)} %get-tuple-element.99.refs_0_, bf16[4096,512]{1,0:T(8,128)(2,1)} %get-tuple-element.85.refs_1_, ...), custom_call_target="tpu_custom_call" | custom-call | flops 32212254720 | bytes 16777216 | tf_op jit(solution)/shard_map/attend_back/pallas_call | solution.py:897
  298.6 34.4 %last_sums.1 = (bf16[2,2,512,512]{3,2,1,0:T(8,128)(2,1)}, bf16[4,208,128]{2,1,0:T(8,128)(2,1)}) custom-call(bf16[2,768,512]{2,1,0:T(8,128)(2,1)} %bitcast.37, f32[4,8,128]{2,1,0:T(8,128)} %get-tuple-element.106.db_ref, f32[8,512]{1,0:T(8,128)} %get-tuple-element.107.sums_ref, f32[512,512]{1,0:T(8,128)} %get-tuple-element.108.dn0_ref, ...), custom_call_target="tpu_custom_call" | custom-call | tf_op jit(solution)/shard_map/last_sums/pallas_call | solution.py:1171
  333.1 5.7 %results.1 = (bf16[2,1024,512]{2,1,0:T(8,128)(2,1)}, bf16[2,1024,512]{2,1,0:T(8,128)(2,1)}, f32[128,256]{1,0:T(8,128)}, f32[128,256]{1,0:T(8,128)}, f32[128,256]...) custom-call(bf16[2,1024,512]{2,1,0:T(8,128)(2,1)} %bitcast.35, ...), custom_call_target="tpu_custom_call" | custom-call | tf_op jit(solution)/shard_map/results/pallas_call | solution.py:1226
  (3 shorter events, 0.0 us)

commit v3 on v2

--- a/solution.py
+++ b/solution.py
@@ -173,11 +173,11 @@
     return [dma((count,)), dma((count,)), dma((count,)), dma((count,)), dma((2,))]
 
 
-def gather_kernel(ns, nc, place, wq_ref, wk_ref, wv_ref, wo_ref, x_block, *refs):
-    tables, (w_out, wo_out, small_out, x_out, small_ref), sems = refs[:-18], refs[-18:-13], refs[-13:]
+def gather_kernel(ns, nc, wq_ref, wk_ref, wv_ref, x_block, *refs):
+    tables, (w_out, small_out, x_out, small_ref), sems = refs[:-17], refs[-17:-13], refs[-13:]
     w_send, w_recv, s_send, s_recv, x_send, x_recv, wt_send, wt_recv, st_send, st_recv, xt_send, xt_recv, local = sems
-    w_refs = (wq_ref, wk_ref, wv_ref, wo_ref)
-    kinds = range(4)
+    w_refs = (wq_ref, wk_ref, wv_ref)
+    kinds = range(3)
     x_ref = x_block.at[0, 0]
     s = lax.axis_index("shard")
     c = lax.axis_index("ctx")
@@ -197,8 +197,6 @@
     greet_wait(peers)
 
     def w_rows(part, kind, owner):
-        if kind == 3:
-            return place(wo_out, part, owner, 0)
         return w_out.at[part, kind, pl.ds(pl.multiple_of(owner * depth, depth), depth), :]
 
     def x_rows(which):
@@ -235,9 +233,9 @@
     last.append(begin(small_ref, small_out.at[1, s], st_send.at[0], st_recv.at[0], {"tp": other}))
     locals_ = [pltpu.make_async_copy(w_refs[k], w_rows(0, k, s), local.at[k]) for k in kinds]
     locals_ += [
-        pltpu.make_async_copy(small_ref, small_out.at[0, s], local.at[4]),
-        pltpu.make_async_copy(x_rows(t), x_out.at[0, 0], local.at[5]),
-        pltpu.make_async_copy(x_rows(other), x_out.at[0, 1], local.at[6]),
+        pltpu.make_async_copy(small_ref, small_out.at[0, s], local.at[3]),
+        pltpu.make_async_copy(x_rows(t), x_out.at[0, 0], local.at[4]),
+        pltpu.make_async_copy(x_rows(other), x_out.at[0, 1], local.at[5]),
     ]
     for copy in locals_:
         copy.start()
@@ -274,7 +272,7 @@
         copy.wait()
 
 
-def gather_first(weights, tables, tokens, place, shape, ns, nc):
+def gather_first(weights, tables, tokens, ns, nc):
     depth, width = weights[0].shape
     length, features = tokens.shape[2:]
     rows = -(-sum(table.shape[0] for table in tables) // 8) * 8
@@ -282,19 +280,18 @@
     dma = pltpu.SemaphoreType.DMA
     vmem = pl.BlockSpec(memory_space=pltpu.VMEM)
     return pl.pallas_call(
-        functools.partial(gather_kernel, ns, nc, place),
+        functools.partial(gather_kernel, ns, nc),
         grid=(1,),
-        in_specs=[vmem] * 4 + [once((1, 1, length, features))] + [vmem] * len(tables),
-        out_specs=[pl.BlockSpec(memory_space=pl.ANY)] * 4,
+        in_specs=[vmem] * 3 + [once((1, 1, length, features))] + [vmem] * len(tables),
+        out_specs=[pl.BlockSpec(memory_space=pl.ANY)] * 3,
         out_shape=[
             jax.ShapeDtypeStruct((2, 3, ns * depth, width), BF16),
-            jax.ShapeDtypeStruct(shape, BF16),
             jax.ShapeDtypeStruct((2, ns, rows, lanes), F32),
             jax.ShapeDtypeStruct((nc, 2, length // 2, features), BF16),
         ],
         scratch_shapes=[pltpu.VMEM((rows, lanes), F32)]
-        + [dma((4, ns)), dma((4, ns)), dma((ns,)), dma((ns,)), dma((nc, 2)), dma((nc, 2))]
-        + [dma((4, ns)), dma((4, ns)), dma((ns,)), dma((ns,)), dma((nc,)), dma((nc,)), dma((7,))],
+        + [dma((3, ns)), dma((3, ns)), dma((ns,)), dma((ns,)), dma((nc, 2)), dma((nc, 2))]
+        + [dma((3, ns)), dma((3, ns)), dma((ns,)), dma((ns,)), dma((nc,)), dma((nc,)), dma((6,))],
         compiler_params=params(collective_id=0, has_side_effects=True),
         name="gather_first",
     )(*weights, tokens, *tables)
@@ -478,11 +475,17 @@
             for h in range(2 if relayed else 0):
                 gather.relay(h).start()
 
-    @pl.when(step == last)
-    def _():
+    def forward_last():
         for gather in gathers("shard"):
-            if not far:
-                gather.forward()
+            gather.forward()
+        for gather in gathers("ctx"):
+            if relayed:
+                gather.forward_relayed()
+            else:
+                gather.forward([far])
+
+    if far:
+        pl.when(step == last)(forward_last)
 
     outs = []
     for h in range(2):
@@ -502,14 +505,8 @@
 
     @pl.when(step == last)
     def _():
-        if far:
-            for gather in gathers("shard"):
-                gather.forward()
-            for gather in gathers("ctx"):
-                if relayed:
-                    gather.forward_relayed()
-                else:
-                    gather.forward([far])
+        if not far:
+            forward_last()
         for name in counts:
             for gather in gathers(name):
                 gather.finish(relayed and name == "ctx")
@@ -553,8 +550,7 @@
 def sum_rows(target, at, left, left_at, right, right_at, rows, chunk=64):
     def one(i, carry):
         here = pl.multiple_of(i * chunk, chunk)
-        value = left[pl.ds(left_at + here, chunk), :].astype(F32) + right[pl.ds(right_at + here, chunk), :].astype(F32)
-        target[pl.ds(at + here, chunk), :] = value.astype(target.dtype)
+        target[pl.ds(at + here, chunk), :] = left[pl.ds(left_at + here, chunk), :] + right[pl.ds(right_at + here, chunk), :]
         return carry
 
     lax.fori_loop(0, rows // chunk, one, 0)
@@ -974,8 +970,8 @@
 
 
 def ffn_kernel(
-    where_ref, x_ref, o0_ref, o1_ref, g_ref, w_out, up_first, up_rest, down_first, down_rest, bup_ref, vec_ref,
-    out_ref, gm_ref, gx_ref, dw_ref, extra_ref, dw_acc, w_up, w_down, dup_ref, dvec_ref, extra, *, ns, up_part,
+    where_ref, x_ref, o0_ref, o1_ref, g_ref, w_out, up_first, up_rest, w_down, bup_ref, vec_ref,
+    out_ref, gm_ref, gx_ref, dw_ref, extra_ref, dw_acc, w_up, dup_ref, dvec_ref, extra, *, ns, up_part,
 ):
     step = pl.program_id(0)
     steps = pl.num_programs(0)
@@ -988,9 +984,6 @@
         split = up_first.shape[2]
         w_up[:, :, :split] = up_first[...]
         w_up[:, :, split:] = up_rest[...]
-        split = down_first.shape[1]
-        w_down[:, :split] = down_first[...]
-        w_down[:, split:] = down_rest[...]
         dw_acc[...] = jnp.zeros_like(dw_acc)
         dup_ref[...] = jnp.zeros_like(dup_ref)
         dvec_ref[...] = jnp.zeros_like(dvec_ref)
@@ -1052,7 +1045,7 @@
     return dot_nn(jnp.broadcast_to(row.astype(BF16), (16, count)), chosen)[0:1]
 
 
-def feed_forward(tokens, mixed, cotangent, w_out, up_first, up_rest, down_first, down_rest, b_up, vectors, where, up_part, ns, nc):
+def feed_forward(tokens, mixed, cotangent, w_out, up_first, up_rest, w_down, b_up, vectors, where, up_part, ns, nc):
     micros, _, length, features = tokens.shape
     block = 256
     half = length // 2
@@ -1074,13 +1067,13 @@
                 pl.BlockSpec((block, 2 * hw), lambda i, t: (jnp.maximum(i - each, 0), 0)),
                 input_spec,
             ]
-            + [once(w.shape) for w in (w_out, up_first, up_rest, down_first, down_rest)]
+            + [once(w.shape) for w in (w_out, up_first, up_rest, w_down)]
             + [once(b_up.shape), once(vectors.shape)],
             out_specs=[row_spec] * 3
             + [once((2, total, features)), full_spec(more)],
             scratch_shapes=[
                 pltpu.VMEM((2, total, features), F32), pltpu.VMEM((2, features, hidden), BF16),
-                pltpu.VMEM((2, hidden, features), BF16), pltpu.VMEM((2, 1, hidden), F32), pltpu.VMEM((8, features), F32),
+                pltpu.VMEM((2, 1, hidden), F32), pltpu.VMEM((8, features), F32),
                 pltpu.VMEM(more, F32),
             ],
         ),
@@ -1096,14 +1089,14 @@
             flops=12 * rows * total * features, bytes_accessed=20 * total * features, transcendentals=4 * rows * hidden
         ),
         name="feed_forward",
-    )(where, tokens, *mixed, cotangent, w_out, up_first, up_rest, down_first, down_rest, b_up, vectors)
+    )(where, tokens, *mixed, cotangent, w_out, up_first, up_rest, w_down, b_up, vectors)
 
 
 def last_kernel(
     dw_ref, db_ref, sums_ref, dn0_ref, dn1_ref, other0_ref, other1_ref, x_ref, gm_ref, vec_ref,
     grad_ref, blocks_ref,
-    extra, extra_ref, dn_received, w_received, w_total, w_blocks, z_parts, z_received,
-    dn_out, dn_in, wtp_out, wtp_in, wctx_out, wctx_in, z_out, z_in, back_out, back_in, row_out, row_in, *, ns, nc, head_part,
+    extra, extra_ref, x_rows, gm_rows, dn_received, w_received, w_total, w_blocks, z_parts, z_received,
+    dn_out, dn_in, wtp_out, wtp_in, wctx_out, wctx_in, z_out, z_in, back_out, back_in, row_out, row_in, fetched, *, ns, nc, head_part,
 ):
     t = lax.axis_index("tp")
     half = grad_ref.shape[2]
@@ -1126,8 +1119,8 @@
 
         def one(i, carry):
             at = pl.multiple_of(i * size, size)
-            unit, inverse = unit_norm(x_ref[micro, 0, pl.ds(t * half + at, size), :].astype(F32))
-            value = gm_ref[micro, pl.ds(at, size), :] + norm_back(
+            unit, inverse = unit_norm(x_rows[micro, pl.ds(at, size), :].astype(F32))
+            value = gm_rows[micro, pl.ds(at, size), :] + norm_back(
                 dn_ref[pl.ds(at, size), :] + dn_received[micro, pl.ds(at, size), :].astype(F32),
                 unit, inverse, vec_ref[2:3],
             )
@@ -1139,6 +1132,12 @@
 
     peers = [("tp", 2), ("ctx", nc), ("shard", ns)]
     greet_first(peers)
+    own = x_ref.at[:, 0, pl.ds(pl.multiple_of(t * half, half), half), :]
+    fetches = [
+        pltpu.make_async_copy(own, x_rows, fetched.at[0]), pltpu.make_async_copy(gm_ref, gm_rows, fetched.at[1])
+    ]
+    for copy in fetches:
+        copy.start()
     features = sums_ref.shape[1]
     each = db_ref.shape[0] // 2
     extra[...] = jnp.zeros_like(extra)
@@ -1152,6 +1151,8 @@
     for copy in others:
         copy.start()
     rows.spread()
+    for copy in fetches:
+        copy.wait()
     finish_rows(0, dn0_ref)
     rows.finish(z_parts)
     weights.start()
@@ -1170,17 +1171,21 @@
     size, part = rows // nc, features // ns
     return pl.pallas_call(
         functools.partial(last_kernel, ns=ns, nc=nc, head_part=head_part),
-        in_specs=[pl.BlockSpec(memory_space=pltpu.VMEM)] * 10,
+        in_specs=[pl.BlockSpec(memory_space=pltpu.VMEM)] * 7
+        + [pl.BlockSpec(memory_space=pl.ANY)] * 2
+        + [pl.BlockSpec(memory_space=pltpu.VMEM)],
         out_specs=[pl.BlockSpec(memory_space=pltpu.VMEM)] * 2,
         out_shape=[
             jax.ShapeDtypeStruct((micros, 2, half, features), BF16),
             jax.ShapeDtypeStruct((nc, size, part), BF16),
         ],
         scratch_shapes=[
-            pltpu.VMEM(more, F32), pltpu.VMEM(more, BF16), pltpu.VMEM((micros, half, features), BF16),
+            pltpu.VMEM(more, F32), pltpu.VMEM(more, BF16),
+            pltpu.VMEM((micros, half, features), BF16), pltpu.VMEM((micros, half, features), F32),
+            pltpu.VMEM((micros, half, features), BF16),
             pltpu.VMEM((rows, features), BF16), pltpu.VMEM((rows, features), BF16), pltpu.VMEM((nc, size, features), BF16),
             pltpu.VMEM((ns, size, part), BF16), pltpu.VMEM((ns, size, part), BF16),
-            *axis_sems(micros, 2, nc, ns, nc, micros),
+            *axis_sems(micros, 2, nc, ns, nc, micros), pltpu.SemaphoreType.DMA((2,)),
         ],
         compiler_params=params(collective_id=5, has_side_effects=True),
         name="last_sums",
@@ -1265,9 +1270,7 @@
             w = w.transpose(0, 2, 1, 3).reshape(2, w.shape[2], features)
         return w
 
-    w_all, wo, small_all, x_first = gather_first(
-        (w_query, w_key, w_value, w_out), tables, tokens, column_place, column_shape(w_out, w_out.shape[0]), ns, nc
-    )
+    w_all, small_all, x_first = gather_first((w_query, w_key, w_value), tables, tokens, ns, nc)
 
     def by_head(row, part):
         table = small_all[:, :, row : row + heads, :part].transpose(0, 2, 1, 3)
@@ -1277,10 +1280,10 @@
     bup = by_head(2 * heads, up_part)[:, None]
     vectors = small_all[0, :, 3 * heads : 3 * heads + 6, :feature_part].transpose(1, 0, 2)
     vectors = vectors.reshape(6, features)
-    ahead, up_ahead = w_down.shape[0] // 4, w_up.shape[1] // 4
+    up_ahead = w_up.shape[1] // 4
     plans = [
         (("ctx", nc, place_distance, True, 0), ("shard", ns, place_rows, False, up_ahead)),
-        (("shard", ns, column_place, False, ahead),),
+        (("shard", ns, column_place, False, 0),),
     ]
     sources = [(tokens, w_up), (w_down,)]
     specs = [
@@ -1289,11 +1292,11 @@
     ]
     shapes = [
         ((nc, 2, half, features), (2, features, w_up.shape[1] - up_ahead)),
-        (column_shape(w_down, w_down.shape[0] - ahead),),
+        (column_shape(w_down, w_down.shape[0]),),
     ]
     guests = [
         (w_up, up_ahead, (2, features, up_ahead), place_rows),
-        (w_down, ahead, column_shape(w_down, ahead), column_place),
+        (w_out, w_out.shape[0], column_shape(w_out, w_out.shape[0]), column_place),
     ]
     x_alls = [x_first.reshape(keys, features), None]
     saved = []
@@ -1311,11 +1314,11 @@
             x_alls[1] = more.pop(0).reshape(keys, features)
         arrived += [early] + more
         saved.append((normed, k, v, qx, mixed))
-    up_first, up_rest, down_first, down_rest = arrived
-    wo, down_first, down_rest = whole_columns(wo), whole_columns(down_first), whole_columns(down_rest)
+    up_first, up_rest, wo, wd = arrived
+    wo, wd = whole_columns(wo), whole_columns(wd)
 
     out, grad_middle, grad_mixed, dw, extra = feed_forward(
-        tokens, [entry[4] for entry in saved], cotangent, wo, up_first, up_rest, down_first, down_rest, bup, vectors,
+        tokens, [entry[4] for entry in saved], cotangent, wo, up_first, up_rest, wd, bup, vectors,
         jnp.full((1,), t, jnp.int32), up_part, ns, nc,
     )
 

time: 340 us -> 333 us (0.979)
  Pallas kernels: 334 us -> 327 us
    pallas_call x2, Pallas kernels: 32.2 us -> 28.8 us  [front(): pl.pallas_call(functools.partial(front_kernel, q_scale=scale, ns=ns, plac...]
where the time goes in v3:
time: 333 us
  Pallas kernels  327 us (98%)
  local copies, waits for them, and re-layouts  3.85 us (1%)
    pallas_call x2, Pallas kernels, attend_back(): pl.pallas_call(functools.partial(attend_back_kernel, width=width, nc=nc,...  145 us
    pallas_call x2, Pallas kernels, attend_forward(): pl.pallas_call(functools.partial(attend_kernel, kc=kc, width=width, plans...  60.5 us
    pallas_call x1, Pallas kernels, last_sums(): pl.pallas_call(functools.partial(last_kernel, ns=ns, nc=nc, head_part=hea...  32.5 us
    pallas_call x2, Pallas kernels, front(): pl.pallas_call(functools.partial(front_kernel, q_scale=scale, ns=ns, plac...  28.8 us
    pallas_call x1, Pallas kernels, gather_first(): pl.pallas_call(functools.partial(gather_kernel, ns, nc), grid=(1,), in_sp...  28 us
    pallas_call x1, Pallas kernels, feed_forward(): pl.pallas_call(functools.partial(ffn_kernel, ns=ns, up_part=up_part), gri...  27 us

profile of v3, /device:TPU:0, one launch (start us, length us, event | category | flops | bytes accessed | tf_op | source)
XLA Modules:
  0.0 332.7 jit_solution(15410212293968107797)
XLA Ops:
  0.7 28.0 %gather_first.1 = (bf16[2,3,512,256]{3,2,1,0:T(8,128)(2,1)}, f32[2,4,24,128]{3,2,1,0:T(8,128)}, bf16[4,2,512,512]{3,2,1,0:T(8,128)(2,1)}) custom-call(bf16[128,256]{1,0:T(8,128)(2,1)} %wq_ref.1, bf16[128,256]{1,0:T(8,128)(2,1)} %wk_ref.1, bf16[128,256]{1,0:T(8,128)(2,1)} %wv_ref.1, bf16[2,1,1024,512]{3,2,1,0:T(8,128)(2,1)} %x_ref.3, bf16[4,16]{1,0:T(4,128)(2,1)} %refs_0_.1, ...), custom_call_target="tpu_custom_call" | custom-call | tf_op jit(solution)/shard_map/gather_first/pallas_call | solution.py:282
  28.7 1.4 slice_bitcast_fusion.3.vec_ref
  30.0 0.8 slice_bitcast_fusion
  30.8 0.8 slice_bitcast_fusion.2
  31.6 0.1 stack_reshape_reshape.6
  31.7 0.7 broadcast_in_dim_reshape.3.bup_ref
  32.4 0.1 stack_reshape_reshape.7
  32.5 0.6 pad_maximum_fusion.bias_ref
  33.1 14.6 %front.2 = (bf16[4096,512]{1,0:T(8,128)(2,1)}, bf16[4096,512]{1,0:T(8,128)(2,1)}, bf16[4096,512]{1,0:T(8,128)(2,1)}, bf16[512,512]{1,0:T(8,128)(2,1)}, bf16[2,512,256]{2,1,0:T(8,128)(2,1)}) custom-call(bf16[4096,512]{1,0:T(8,128)(2,1)} %bitcast.46, bf16[2,3,512,256]{3,2,1,0:T(8,128)(2,1)} %get-tuple-element.75.w_ref.refs_7_, ...), custom_call_target="tpu_custom_call" | custom-call | flops 4294967296 | bytes 16777216 | tf_op jit(solution)/shard_map/front/pallas_call | solution.py:358
  47.8 31.3 %attend_forward.2 = (bf16[512,512]{1,0:T(8,128)(2,1)}, bf16[512,1024]{1,0:T(8,128)(2,1)}, bf16[4,2,512,512]{3,2,1,0:T(8,128)(2,1)}, bf16[2,512,768]{2,1,0:T(8,128)(2,1)}) custom-call(bf16[512,512]{1,0:T(8,128)(2,1)} %get-tuple-element.77.refs_0_, bf16[4096,512]{1,0:T(8,128)(2,1)} %get-tuple-element.78.refs_1_, bf16[4096,512]{1,0:T(8,128)(2,1)} %get-tuple-element.79.refs_2_, ...), custom_call_target="tpu_custom_call" | custom-call | flops 12884901888 | bytes 8388608 | tf_op jit(solution)/shard_map/attend_forward/pallas_call | solution.py:521
  79.1 14.1 %front.3 = (bf16[4096,512]{1,0:T(8,128)(2,1)}, bf16[4096,512]{1,0:T(8,128)(2,1)}, bf16[4096,512]{1,0:T(8,128)(2,1)}, bf16[512,512]{1,0:T(8,128)(2,1)}, bf16[2,256,512]{2,1,0:T(8,128)(2,1)}) custom-call(bf16[4096,512]{1,0:T(8,128)(2,1)} %bitcast.50, bf16[2,3,512,256]{3,2,1,0:T(8,128)(2,1)} %get-tuple-element.75.w_ref.refs_7_, ...), custom_call_target="tpu_custom_call" | custom-call | flops 4294967296 | bytes 16777216 | tf_op jit(solution)/shard_map/front/pallas_call | solution.py:358
  93.2 29.3 %attend_forward.3 = (bf16[512,512]{1,0:T(8,128)(2,1)}, bf16[512,1024]{1,0:T(8,128)(2,1)}, bf16[2,1024,512]{2,1,0:T(8,128)(2,1)}) custom-call(bf16[512,512]{1,0:T(8,128)(2,1)} %get-tuple-element.83.refs_0_, bf16[4096,512]{1,0:T(8,128)(2,1)} %get-tuple-element.84.refs_1_, bf16[4096,512]{1,0:T(8,128)(2,1)} %get-tuple-element.85.refs_2_, bf16[1024,128]{1,0:T(8,128)(2,1)} %refs_3_.3), custom_call_target="tpu_custom_call" | custom-call | flops 12884901888 | bytes 8388608 | tf_op jit(solution)/shard_map/attend_forward/pallas_call | solution.py:521
  122.5 27.0 %feed_forward.1 = (bf16[1024,512]{1,0:T(8,128)(2,1)}, f32[1024,512]{1,0:T(8,128)}, bf16[1024,512]{1,0:T(8,128)(2,1)}, bf16[2,2304,512]{2,1,0:T(8,128)(2,1)}, bf16[2,64,512]{2,1,0:T(8,128)(2,1)}) custom-call(s32[1]{0:T(128)} %bitcast.12.where_ref, bf16[2,1,1024,512]{3,2,1,0:T(8,128)(2,1)} %x_ref.3, bf16[512,512]{1,0:T(8,128)(2,1)} %get-tuple-element.81.o0_ref.refs_4_, ...), custom_call_target="tpu_custom_call" | custom-call | flops 14495514624 | bytes 23592960 | tf_op jit(solution)/shard_map/feed_forward/pallas_call | solution.py:1059
  149.4 73.6 %attend_back.2 = (f32[4,3,128,512]{3,2,1,0:T(8,128)}, f32[4,8,128]{2,1,0:T(8,128)}, f32[8,512]{1,0:T(8,128)}, f32[512,512]{1,0:T(8,128)}, bf16[512,512]{1,0:T(8,...) custom-call(bf16[512,1024]{1,0:T(8,128)(2,1)} %get-tuple-element.80.refs_0_, ...), custom_call_target="tpu_custom_call" | custom-call | flops 32212254720 | bytes 16777216 | tf_op jit(solution)/shard_map/attend_back/pallas_call | solution.py:893
  223.1 71.3 %attend_back.3 = (bf16[4,3,128,512]{3,2,1,0:T(8,128)(2,1)}, f32[4,8,128]{2,1,0:T(8,128)}, f32[8,512]{1,0:T(8,128)}, f32[512,512]{1,0:T(8,128)}, bf16[512,512]{1,0:T(8,128)(2,1)}, /*index=5*/bf16[4,592,128]{2,1,0:T(8,128)(2,1)}) custom-call(bf16[512,1024]{1,0:T(8,128)(2,1)} %get-tuple-element.97.refs_0_, bf16[4096,512]{1,0:T(8,128)(2,1)} %get-tuple-element.84.refs_1_, ...), custom_call_target="tpu_custom_call" | custom-call | flops 32212254720 | bytes 16777216 | tf_op jit(solution)/shard_map/attend_back/pallas_call | solution.py:893
  294.4 32.5 %last_sums.1 = (bf16[2,2,512,512]{3,2,1,0:T(8,128)(2,1)}, bf16[4,208,128]{2,1,0:T(8,128)(2,1)}) custom-call(bf16[2,768,512]{2,1,0:T(8,128)(2,1)} %bitcast.37, f32[4,8,128]{2,1,0:T(8,128)} %get-tuple-element.104.db_ref, f32[8,512]{1,0:T(8,128)} %get-tuple-element.105.sums_ref, f32[512,512]{1,0:T(8,128)} %get-tuple-element.106.dn0_ref, ...), custom_call_target="tpu_custom_call" | custom-call | tf_op jit(solution)/shard_map/last_sums/pallas_call | solution.py:1172
  326.9 5.7 %results.1 = (bf16[2,1024,512]{2,1,0:T(8,128)(2,1)}, bf16[2,1024,512]{2,1,0:T(8,128)(2,1)}, f32[128,256]{1,0:T(8,128)}, f32[128,256]{1,0:T(8,128)}, f32[128,256]...) custom-call(bf16[2,1024,512]{2,1,0:T(8,128)(2,1)} %bitcast.35, ...), custom_call_target="tpu_custom_call" | custom-call | tf_op jit(solution)/shard_map/results/pallas_call | solution.py:1231
  (3 shorter events, 0.0 us)

commit v4 on v3

--- a/solution.py
+++ b/solution.py
@@ -125,14 +125,40 @@
             self.first(d).wait_recv()
             self.cross(d).start()
 
+    def half(self, d, h):
+        size = self.source.shape[0] // 2
+        rows = pl.ds(h * size, size)
+        i = d + h * self.count
+        return send(
+            self.source.at[rows, :], self.target.at[d, 0, rows, :], self.out_sem.at[i], self.in_sem.at[i],
+            {self.name: self.me ^ d},
+        )
+
     def relay(self, h):
-        size = self.target.shape[2] // 2
+        size = self.source.shape[0] // 2
         rows = pl.ds(h * size, size)
-        i = (3, 0)[h]
-        where = {self.name: self.me ^ (2 - h)}
+        i = 3 + h * self.count
         return send(
-            self.target.at[1 + h, 0, rows, :], self.target.at[3, 0, rows, :], self.out_sem.at[i], self.in_sem.at[i], where
+            self.target.at[1 + h, 0, rows, :], self.target.at[3, 0, rows, :], self.out_sem.at[i], self.in_sem.at[i],
+            {self.name: self.me ^ (2 - h)},
         )
+
+    def start_relayed(self):
+        for h in range(2):
+            for d in (1, 2):
+                self.half(d, h if d == 1 else 1 - h).start()
+        for copy in self.locals():
+            copy.start()
+
+    def pass_on(self):
+        for h in range(2):
+            self.half(1 + h, h).wait_recv()
+            self.relay(h).start()
+
+    def forward_near(self):
+        for d in (1, 2):
+            self.half(d, 1 if d == 1 else 0).wait_recv()
+            self.cross(d).start()
 
     def forward_relayed(self):
         for h in range(2):
@@ -140,10 +166,14 @@
         self.cross(3).start()
 
     def finish(self, relayed=False):
-        for d in range(1, 3 if relayed else self.count):
-            self.first(d).wait_send()
-        for h in range(2 if relayed else 0):
-            self.relay(h).wait_send()
+        if relayed:
+            for h in range(2):
+                for d in (1, 2):
+                    self.half(d, h).wait_send()
+                self.relay(h).wait_send()
+        else:
+            for d in range(1, self.count):
+                self.first(d).wait_send()
         for d in self.crossed():
             self.cross(d).wait()
         for copy in self.locals():
@@ -170,11 +200,11 @@
 
 def gather_sems(count):
     dma = pltpu.SemaphoreType.DMA
-    return [dma((count,)), dma((count,)), dma((count,)), dma((count,)), dma((2,))]
+    return [dma((2 * count,)), dma((2 * count,)), dma((count,)), dma((count,)), dma((2,))]
 
 
 def gather_kernel(ns, nc, wq_ref, wk_ref, wv_ref, x_block, *refs):
-    tables, (w_out, small_out, x_out, small_ref), sems = refs[:-17], refs[-17:-13], refs[-13:]
+    tables, (w_out, x_out, vec_out, bias_out, bup_out, small_ref, small_out), sems = refs[:-20], refs[-20:-13], refs[-13:]
     w_send, w_recv, s_send, s_recv, x_send, x_recv, wt_send, wt_recv, st_send, st_recv, xt_send, xt_recv, local = sems
     w_refs = (wq_ref, wk_ref, wv_ref)
     kinds = range(3)
@@ -270,6 +300,25 @@
         copy.wait()
     for copy in locals_:
         copy.wait()
+    heads = tables[0].shape[0]
+    vec_out[...] = jnp.zeros_like(vec_out)
+    bias_out[...] = jnp.zeros_like(bias_out)
+    for shard in range(ns):
+        width = tables[3].shape[1]
+        for i in range(len(tables) - 3):
+            row = small_out[0, shard, 3 * heads + i : 3 * heads + i + 1, :width]
+            vec_out[i : i + 1, shard * width : (shard + 1) * width] = row
+        for which in range(3):
+            width = tables[which].shape[1]
+            for part in range(2):
+                for h in range(heads):
+                    row = small_out[part, shard, which * heads + h : which * heads + h + 1, :width]
+                    at = (h * ns + shard) * width
+                    if which == 2:
+                        bup_out[part, :, at : at + width] = row
+                    else:
+                        at += part * heads * ns * width
+                        bias_out[which : which + 1, at : at + width] = row
 
 
 def gather_first(weights, tables, tokens, ns, nc):
@@ -277,19 +326,20 @@
     length, features = tokens.shape[2:]
     rows = -(-sum(table.shape[0] for table in tables) // 8) * 8
     lanes = -(-max(table.shape[1] for table in tables) // 128) * 128
+    finals = [(8, features), (8, 2 * tables[0].size * ns), (2, 1, tables[2].size * ns)]
     dma = pltpu.SemaphoreType.DMA
     vmem = pl.BlockSpec(memory_space=pltpu.VMEM)
     return pl.pallas_call(
         functools.partial(gather_kernel, ns, nc),
         grid=(1,),
         in_specs=[vmem] * 3 + [once((1, 1, length, features))] + [vmem] * len(tables),
-        out_specs=[pl.BlockSpec(memory_space=pl.ANY)] * 3,
+        out_specs=[pl.BlockSpec(memory_space=pl.ANY)] * 2 + [full_spec(shape) for shape in finals],
         out_shape=[
             jax.ShapeDtypeStruct((2, 3, ns * depth, width), BF16),
-            jax.ShapeDtypeStruct((2, ns, rows, lanes), F32),
             jax.ShapeDtypeStruct((nc, 2, length // 2, features), BF16),
-        ],
-        scratch_shapes=[pltpu.VMEM((rows, lanes), F32)]
+        ]
+        + [jax.ShapeDtypeStruct(shape, F32) for shape in finals],
+        scratch_shapes=[pltpu.VMEM((rows, lanes), F32), pltpu.VMEM((2, ns, rows, lanes), F32)]
         + [dma((3, ns)), dma((3, ns)), dma((ns,)), dma((ns,)), dma((nc, 2)), dma((nc, 2))]
         + [dma((3, ns)), dma((3, ns)), dma((ns,)), dma((ns,)), dma((nc,)), dma((nc,)), dma((6,))],
         compiler_params=params(collective_id=0, has_side_effects=True),
@@ -464,16 +514,25 @@
         for gather in gathers("shard"):
             gather.start()
         for gather in gathers("ctx"):
-            gather.start(1)
+            if relayed:
+                gather.start_relayed()
+            else:
+                gather.start(1)
+
+    @pl.when(step == 1)
+    def _():
+        for gather in gathers("ctx"):
+            if relayed:
+                gather.pass_on()
 
     @pl.when(step == 2)
     def _():
         for gather in gathers("ctx"):
-            if not relayed:
+            if relayed:
+                gather.forward_near()
+            else:
                 gather.first(far).start()
-            gather.forward(range(1, far))
-            for h in range(2 if relayed else 0):
-                gather.relay(h).start()
+                gather.forward(range(1, far))
 
     def forward_last():
         for gather in gathers("shard"):
@@ -1270,16 +1329,8 @@
             w = w.transpose(0, 2, 1, 3).reshape(2, w.shape[2], features)
         return w
 
-    w_all, small_all, x_first = gather_first((w_query, w_key, w_value), tables, tokens, ns, nc)
-
-    def by_head(row, part):
-        table = small_all[:, :, row : row + heads, :part].transpose(0, 2, 1, 3)
-        return table.reshape(2, heads * part * ns)
-
-    biases = jnp.stack([by_head(0, head_part).reshape(-1), by_head(heads, head_part).reshape(-1)])
-    bup = by_head(2 * heads, up_part)[:, None]
-    vectors = small_all[0, :, 3 * heads : 3 * heads + 6, :feature_part].transpose(1, 0, 2)
-    vectors = vectors.reshape(6, features)
+    w_all, x_first, vectors, biases, bup = gather_first((w_query, w_key, w_value), tables, tokens, ns, nc)
+
     up_ahead = w_up.shape[1] // 4
     plans = [
         (("ctx", nc, place_distance, True, 0), ("shard", ns, place_rows, False, up_ahead)),

time: 333 us -> 330 us (level)
  local copies, waits for them, and re-layouts: 3.85 us -> 0 us
where the time goes in v4:
time: 330 us; the launch traced here: 329 us
  Pallas kernels  328 us (99%)
    pallas_call x2, Pallas kernels, attend_back(): pl.pallas_call(functools.partial(attend_back_kernel, width=width, nc=nc,...  145 us
    pallas_call x2, Pallas kernels, attend_forward(): pl.pallas_call(functools.partial(attend_kernel, kc=kc, width=width, plans...  59.5 us
    pallas_call x1, Pallas kernels, last_sums(): pl.pallas_call(functools.partial(last_kernel, ns=ns, nc=nc, head_part=hea...  33.2 us
    pallas_call x2, Pallas kernels, front(): pl.pallas_call(functools.partial(front_kernel, q_scale=scale, ns=ns, plac...  29.1 us
    pallas_call x1, Pallas kernels, gather_first(): pl.pallas_call(functools.partial(gather_kernel, ns, nc), grid=(1,), in_sp...  28.7 us
    pallas_call x1, Pallas kernels, feed_forward(): pl.pallas_call(functools.partial(ffn_kernel, ns=ns, up_part=up_part), gri...  27 us

profile of v4, /device:TPU:0, one launch (start us, length us, event | category | flops | bytes accessed | tf_op | source)
XLA Modules:
  0.0 329.2 jit_solution(1458599282006645656)
XLA Ops:
  0.7 28.7 %gather_first.1 = (bf16[2,3,512,256]{3,2,1,0:T(8,128)(2,1)}, bf16[4,2,512,512]{3,2,1,0:T(8,128)(2,1)}, f32[8,512]{1,0:T(8,128)}, f32[8,512]{1,0:T(8,128)}, f32[2,1,1024]{2,1,0:T(1,128)}) custom-call(bf16[128,256]{1,0:T(8,128)(2,1)} %wq_ref.1, bf16[128,256]{1,0:T(8,128)(2,1)} %wk_ref.1, bf16[128,256]{1,0:T(8,128)(2,1)} %wv_ref.1, ...), custom_call_target="tpu_custom_call" | custom-call | tf_op jit(solution)/shard_map/gather_first/pallas_call | solution.py:332
  29.4 14.7 %front.2 = (bf16[4096,512]{1,0:T(8,128)(2,1)}, bf16[4096,512]{1,0:T(8,128)(2,1)}, bf16[4096,512]{1,0:T(8,128)(2,1)}, bf16[512,512]{1,0:T(8,128)(2,1)}, bf16[2,512,256]{2,1,0:T(8,128)(2,1)}) custom-call(bf16[4096,512]{1,0:T(8,128)(2,1)} %bitcast.34, bf16[2,3,512,256]{3,2,1,0:T(8,128)(2,1)} %get-tuple-element.77.w_ref.refs_7_, ...), custom_call_target="tpu_custom_call" | custom-call | flops 4294967296 | bytes 16777216 | tf_op jit(solution)/shard_map/front/pallas_call | solution.py:408
  44.1 30.2 %attend_forward.2 = (bf16[512,512]{1,0:T(8,128)(2,1)}, bf16[512,1024]{1,0:T(8,128)(2,1)}, bf16[4,2,512,512]{3,2,1,0:T(8,128)(2,1)}, bf16[2,512,768]{2,1,0:T(8,128)(2,1)}) custom-call(bf16[512,512]{1,0:T(8,128)(2,1)} %get-tuple-element.80.refs_0_, bf16[4096,512]{1,0:T(8,128)(2,1)} %get-tuple-element.81.refs_1_, bf16[4096,512]{1,0:T(8,128)(2,1)} %get-tuple-element.82.refs_2_, ...), custom_call_target="tpu_custom_call" | custom-call | flops 12884901888 | bytes 8388608 | tf_op jit(solution)/shard_map/attend_forward/pallas_call | solution.py:580
  74.3 14.4 %front.3 = (bf16[4096,512]{1,0:T(8,128)(2,1)}, bf16[4096,512]{1,0:T(8,128)(2,1)}, bf16[4096,512]{1,0:T(8,128)(2,1)}, bf16[512,512]{1,0:T(8,128)(2,1)}, bf16[2,256,512]{2,1,0:T(8,128)(2,1)}) custom-call(bf16[4096,512]{1,0:T(8,128)(2,1)} %bitcast.38, bf16[2,3,512,256]{3,2,1,0:T(8,128)(2,1)} %get-tuple-element.77.w_ref.refs_7_, ...), custom_call_target="tpu_custom_call" | custom-call | flops 4294967296 | bytes 16777216 | tf_op jit(solution)/shard_map/front/pallas_call | solution.py:408
  88.7 29.3 %attend_forward.3 = (bf16[512,512]{1,0:T(8,128)(2,1)}, bf16[512,1024]{1,0:T(8,128)(2,1)}, bf16[2,1024,512]{2,1,0:T(8,128)(2,1)}) custom-call(bf16[512,512]{1,0:T(8,128)(2,1)} %get-tuple-element.86.refs_0_, bf16[4096,512]{1,0:T(8,128)(2,1)} %get-tuple-element.87.refs_1_, bf16[4096,512]{1,0:T(8,128)(2,1)} %get-tuple-element.88.refs_2_, bf16[1024,128]{1,0:T(8,128)(2,1)} %refs_3_.3), custom_call_target="tpu_custom_call" | custom-call | flops 12884901888 | bytes 8388608 | tf_op jit(solution)/shard_map/attend_forward/pallas_call | solution.py:580
  118.1 27.0 %feed_forward.1 = (bf16[1024,512]{1,0:T(8,128)(2,1)}, f32[1024,512]{1,0:T(8,128)}, bf16[1024,512]{1,0:T(8,128)(2,1)}, bf16[2,2304,512]{2,1,0:T(8,128)(2,1)}, bf16[2,64,512]{2,1,0:T(8,128)(2,1)}) custom-call(s32[1]{0:T(128)} %bitcast.7.where_ref, bf16[2,1,1024,512]{3,2,1,0:T(8,128)(2,1)} %x_ref.3, bf16[512,512]{1,0:T(8,128)(2,1)} %get-tuple-element.84.o0_ref.refs_4_, ...), custom_call_target="tpu_custom_call" | custom-call | flops 14495514624 | bytes 23592960 | tf_op jit(solution)/shard_map/feed_forward/pallas_call | solution.py:1118
  145.1 73.6 %attend_back.2 = (f32[4,3,128,512]{3,2,1,0:T(8,128)}, f32[4,8,128]{2,1,0:T(8,128)}, f32[8,512]{1,0:T(8,128)}, f32[512,512]{1,0:T(8,128)}, bf16[512,512]{1,0:T(8,...) custom-call(bf16[512,1024]{1,0:T(8,128)(2,1)} %get-tuple-element.83.refs_0_, ...), custom_call_target="tpu_custom_call" | custom-call | flops 32212254720 | bytes 16777216 | tf_op jit(solution)/shard_map/attend_back/pallas_call | solution.py:952
  218.7 71.3 %attend_back.3 = (bf16[4,3,128,512]{3,2,1,0:T(8,128)(2,1)}, f32[4,8,128]{2,1,0:T(8,128)}, f32[8,512]{1,0:T(8,128)}, f32[512,512]{1,0:T(8,128)}, bf16[512,512]{1,0:T(8,128)(2,1)}, /*index=5*/bf16[4,592,128]{2,1,0:T(8,128)(2,1)}) custom-call(bf16[512,1024]{1,0:T(8,128)(2,1)} %get-tuple-element.101.refs_0_, bf16[4096,512]{1,0:T(8,128)(2,1)} %get-tuple-element.87.refs_1_, ...), custom_call_target="tpu_custom_call" | custom-call | flops 32212254720 | bytes 16777216 | tf_op jit(solution)/shard_map/attend_back/pallas_call | solution.py:952
  290.0 33.2 %last_sums.1 = (bf16[2,2,512,512]{3,2,1,0:T(8,128)(2,1)}, bf16[4,208,128]{2,1,0:T(8,128)(2,1)}) custom-call(bf16[2,768,512]{2,1,0:T(8,128)(2,1)} %bitcast.25, f32[4,8,128]{2,1,0:T(8,128)} %get-tuple-element.108.db_ref, f32[8,512]{1,0:T(8,128)} %get-tuple-element.109.sums_ref, f32[512,512]{1,0:T(8,128)} %get-tuple-element.110.dn0_ref, ...), custom_call_target="tpu_custom_call" | custom-call | tf_op jit(solution)/shard_map/last_sums/pallas_call | solution.py:1231
  323.3 5.7 %results.1 = (bf16[2,1024,512]{2,1,0:T(8,128)(2,1)}, bf16[2,1024,512]{2,1,0:T(8,128)(2,1)}, f32[128,256]{1,0:T(8,128)}, f32[128,256]{1,0:T(8,128)}, f32[128,256]...) custom-call(bf16[2,1024,512]{2,1,0:T(8,128)(2,1)} %bitcast.23, ...), custom_call_target="tpu_custom_call" | custom-call | tf_op jit(solution)/shard_map/results/pallas_call | solution.py:1290

commit v5 on v4

--- a/solution.py
+++ b/solution.py
@@ -841,7 +841,7 @@
         greet_wait(guest.peers)
         guest.begin()
 
-    @pl.when((i == 1) & (j == 0))
+    @pl.when((i == 1) & (j == 2))
     def _():
         guest.middle()
 

time: 330 us -> 330 us (level)
  no operation moved by 1% of the time
where the time goes in v5:
time: 330 us
  Pallas kernels  329 us (100%)
    pallas_call x2, Pallas kernels, attend_back(): pl.pallas_call(functools.partial(attend_back_kernel, width=width, nc=nc,...  146 us
    pallas_call x2, Pallas kernels, attend_forward(): pl.pallas_call(functools.partial(attend_kernel, kc=kc, width=width, plans...  59.5 us
    pallas_call x1, Pallas kernels, last_sums(): pl.pallas_call(functools.partial(last_kernel, ns=ns, nc=nc, head_part=hea...  32.8 us
    pallas_call x2, Pallas kernels, front(): pl.pallas_call(functools.partial(front_kernel, q_scale=scale, ns=ns, plac...  29.1 us
    pallas_call x1, Pallas kernels, gather_first(): pl.pallas_call(functools.partial(gather_kernel, ns, nc), grid=(1,), in_sp...  28.7 us
    pallas_call x1, Pallas kernels, feed_forward(): pl.pallas_call(functools.partial(ffn_kernel, ns=ns, up_part=up_part), gri...  27 us

profile of v5, /device:TPU:0, one launch (start us, length us, event | category | flops | bytes accessed | tf_op | source)
XLA Modules:
  0.0 329.7 jit_solution(614411698267997708)
XLA Ops:
  0.7 28.7 %gather_first.1 = (bf16[2,3,512,256]{3,2,1,0:T(8,128)(2,1)}, bf16[4,2,512,512]{3,2,1,0:T(8,128)(2,1)}, f32[8,512]{1,0:T(8,128)}, f32[8,512]{1,0:T(8,128)}, f32[2,1,1024]{2,1,0:T(1,128)}) custom-call(bf16[128,256]{1,0:T(8,128)(2,1)} %wq_ref.1, bf16[128,256]{1,0:T(8,128)(2,1)} %wk_ref.1, bf16[128,256]{1,0:T(8,128)(2,1)} %wv_ref.1, ...), custom_call_target="tpu_custom_call" | custom-call | tf_op jit(solution)/shard_map/gather_first/pallas_call | solution.py:332
  29.4 14.7 %front.2 = (bf16[4096,512]{1,0:T(8,128)(2,1)}, bf16[4096,512]{1,0:T(8,128)(2,1)}, bf16[4096,512]{1,0:T(8,128)(2,1)}, bf16[512,512]{1,0:T(8,128)(2,1)}, bf16[2,512,256]{2,1,0:T(8,128)(2,1)}) custom-call(bf16[4096,512]{1,0:T(8,128)(2,1)} %bitcast.34, bf16[2,3,512,256]{3,2,1,0:T(8,128)(2,1)} %get-tuple-element.77.w_ref.refs_7_, ...), custom_call_target="tpu_custom_call" | custom-call | flops 4294967296 | bytes 16777216 | tf_op jit(solution)/shard_map/front/pallas_call | solution.py:408
  44.1 30.2 %attend_forward.2 = (bf16[512,512]{1,0:T(8,128)(2,1)}, bf16[512,1024]{1,0:T(8,128)(2,1)}, bf16[4,2,512,512]{3,2,1,0:T(8,128)(2,1)}, bf16[2,512,768]{2,1,0:T(8,128)(2,1)}) custom-call(bf16[512,512]{1,0:T(8,128)(2,1)} %get-tuple-element.80.refs_0_, bf16[4096,512]{1,0:T(8,128)(2,1)} %get-tuple-element.81.refs_1_, bf16[4096,512]{1,0:T(8,128)(2,1)} %get-tuple-element.82.refs_2_, ...), custom_call_target="tpu_custom_call" | custom-call | flops 12884901888 | bytes 8388608 | tf_op jit(solution)/shard_map/attend_forward/pallas_call | solution.py:580
  74.3 14.4 %front.3 = (bf16[4096,512]{1,0:T(8,128)(2,1)}, bf16[4096,512]{1,0:T(8,128)(2,1)}, bf16[4096,512]{1,0:T(8,128)(2,1)}, bf16[512,512]{1,0:T(8,128)(2,1)}, bf16[2,256,512]{2,1,0:T(8,128)(2,1)}) custom-call(bf16[4096,512]{1,0:T(8,128)(2,1)} %bitcast.38, bf16[2,3,512,256]{3,2,1,0:T(8,128)(2,1)} %get-tuple-element.77.w_ref.refs_7_, ...), custom_call_target="tpu_custom_call" | custom-call | flops 4294967296 | bytes 16777216 | tf_op jit(solution)/shard_map/front/pallas_call | solution.py:408
  88.7 29.3 %attend_forward.3 = (bf16[512,512]{1,0:T(8,128)(2,1)}, bf16[512,1024]{1,0:T(8,128)(2,1)}, bf16[2,1024,512]{2,1,0:T(8,128)(2,1)}) custom-call(bf16[512,512]{1,0:T(8,128)(2,1)} %get-tuple-element.86.refs_0_, bf16[4096,512]{1,0:T(8,128)(2,1)} %get-tuple-element.87.refs_1_, bf16[4096,512]{1,0:T(8,128)(2,1)} %get-tuple-element.88.refs_2_, bf16[1024,128]{1,0:T(8,128)(2,1)} %refs_3_.3), custom_call_target="tpu_custom_call" | custom-call | flops 12884901888 | bytes 8388608 | tf_op jit(solution)/shard_map/attend_forward/pallas_call | solution.py:580
  118.1 27.0 %feed_forward.1 = (bf16[1024,512]{1,0:T(8,128)(2,1)}, f32[1024,512]{1,0:T(8,128)}, bf16[1024,512]{1,0:T(8,128)(2,1)}, bf16[2,2304,512]{2,1,0:T(8,128)(2,1)}, bf16[2,64,512]{2,1,0:T(8,128)(2,1)}) custom-call(s32[1]{0:T(128)} %bitcast.7.where_ref, bf16[2,1,1024,512]{3,2,1,0:T(8,128)(2,1)} %x_ref.3, bf16[512,512]{1,0:T(8,128)(2,1)} %get-tuple-element.84.o0_ref.refs_4_, ...), custom_call_target="tpu_custom_call" | custom-call | flops 14495514624 | bytes 23592960 | tf_op jit(solution)/shard_map/feed_forward/pallas_call | solution.py:1118
  145.1 76.9 %attend_back.2 = (f32[4,3,128,512]{3,2,1,0:T(8,128)}, f32[4,8,128]{2,1,0:T(8,128)}, f32[8,512]{1,0:T(8,128)}, f32[512,512]{1,0:T(8,128)}, bf16[512,512]{1,0:T(8,...) custom-call(bf16[512,1024]{1,0:T(8,128)(2,1)} %get-tuple-element.83.refs_0_, ...), custom_call_target="tpu_custom_call" | custom-call | flops 32212254720 | bytes 16777216 | tf_op jit(solution)/shard_map/attend_back/pallas_call | solution.py:952
  222.0 69.0 %attend_back.3 = (bf16[4,3,128,512]{3,2,1,0:T(8,128)(2,1)}, f32[4,8,128]{2,1,0:T(8,128)}, f32[8,512]{1,0:T(8,128)}, f32[512,512]{1,0:T(8,128)}, bf16[512,512]{1,0:T(8,128)(2,1)}, /*index=5*/bf16[4,592,128]{2,1,0:T(8,128)(2,1)}) custom-call(bf16[512,1024]{1,0:T(8,128)(2,1)} %get-tuple-element.101.refs_0_, bf16[4096,512]{1,0:T(8,128)(2,1)} %get-tuple-element.87.refs_1_, ...), custom_call_target="tpu_custom_call" | custom-call | flops 32212254720 | bytes 16777216 | tf_op jit(solution)/shard_map/attend_back/pallas_call | solution.py:952
  291.0 32.8 %last_sums.1 = (bf16[2,2,512,512]{3,2,1,0:T(8,128)(2,1)}, bf16[4,208,128]{2,1,0:T(8,128)(2,1)}) custom-call(bf16[2,768,512]{2,1,0:T(8,128)(2,1)} %bitcast.25, f32[4,8,128]{2,1,0:T(8,128)} %get-tuple-element.108.db_ref, f32[8,512]{1,0:T(8,128)} %get-tuple-element.109.sums_ref, f32[512,512]{1,0:T(8,128)} %get-tuple-element.110.dn0_ref, ...), custom_call_target="tpu_custom_call" | custom-call | tf_op jit(solution)/shard_map/last_sums/pallas_call | solution.py:1231
  323.8 5.7 %results.1 = (bf16[2,1024,512]{2,1,0:T(8,128)(2,1)}, bf16[2,1024,512]{2,1,0:T(8,128)(2,1)}, f32[128,256]{1,0:T(8,128)}, f32[128,256]{1,0:T(8,128)}, f32[128,256]...) custom-call(bf16[2,1024,512]{2,1,0:T(8,128)(2,1)} %bitcast.23, ...), custom_call_target="tpu_custom_call" | custom-call | tf_op jit(solution)/shard_map/results/pallas_call | solution.py:1290
